TPU v7x, 128 devices: a whole 4x4x4 slice. The times are simulated.
128 devices in a mesh: seq: 64 (over y_lo, x, z, core), fsdp: 2 (over y_hi).
Axes of the slice: x: 4, y: 4 (y_hi: 2, y_lo: 2; y = y_hi * 2 + y_lo), z: 4, core: 2. Of those that a mesh axis runs over, the one named last changes fastest.
Arguments:
- state_in: bfloat16 [8192, 5280], P('seq'), may hold values from -6 to 6
- query_vectors: bfloat16 [8192, 2688], P('seq', 'fsdp'), may hold values from -6 to 6
- key_vectors: bfloat16 [8192, 2688], P('seq', 'fsdp'), may hold values from -6 to 6
- value_weight: bfloat16 [2, 1344, 5280], P('fsdp', 'seq'), may hold values from -0.078125 to 0.078125
- out_weight: bfloat16 [2, 1344, 5280], P('fsdp', 'seq'), may hold values from -0.3125 to 0.3125
- doc_ids: int32 [64], replicated, may hold values from 0 to 20, never falling along the last dimension, each value on 1 to 5 neighbouring positions
- cotangent: bfloat16 [8192, 5280], P('seq'), may hold values from -6 to 6
Outputs:
- final_state: bfloat16 [8192, 5280], P('seq')
- state_grad: float32 [8192, 5280], P('seq')
Inputs may be any that keep to these rules, and one draw needn't show every extreme that they name: `doc_ids`: document ids never fall along the blocks; each document covers 1 to 5 consecutive blocks, and some document covers exactly 5.
All inputs are finite; a program needn't handle non-finite values.
Results may differ from a plain program's by a relative error of at most 0.013.
Values may be sent and summed in bfloat16 or wider, within the bound.
No kernel may reach another device: no remote copies, remote signals or barrier semaphores. Data moves between devices by JAX's collectives and lax.ppermute only.
A program may use at most 256 MiB of HBM per device.

v0:
```python
import math

import jax
import jax.numpy as jnp
from jax import lax
from jax.sharding import PartitionSpec as P

HEAD_DIM = 96
BLOCK = 128
UNROLL = 2
REACH = 4


epsilon = 1e-06


def from_everyone(x, axis):
    size = lax.axis_size(axis)
    return lax.all_to_all(jnp.broadcast_to(x[None], (size, *x.shape)), axis, 0, 0, tiled=True)


def taken_together(x, axis):
    everything = from_everyone(x, axis)
    return jnp.sum(everything.astype(jnp.float32), axis=0)


def from_behind(value, axis, steps):
    count = lax.axis_size(axis)
    first, last = (max(0, -steps), min(count, count - steps))
    return lax.ppermute(value, axis, [(source, source + steps) for source in range(first, last)])


def in_one_piece(arrays, axis, dim, along):
    ends, at = ([], 0)
    for a in arrays[:-1]:
        at += a.shape[along]
        ends.append(at)
    both = jnp.concatenate(arrays, axis=along)
    return tuple(jnp.split(lax.all_gather(both, axis, axis=dim, tiled=True), ends, axis=along))


def normalize(current):
    mean_square = jnp.mean(current * current, axis=-1, keepdims=True)
    inverse_rms = lax.rsqrt(mean_square + epsilon)
    return (current * inverse_rms, inverse_rms)


def head_total(partial_value):
    return taken_together(partial_value.astype(jnp.bfloat16), "fsdp").astype(jnp.float32)


def contract_last(left, right):
    return lax.dot_general(
        left, right, (((1,), (1,)), ((), ())), preferred_element_type=jnp.float32
    )


def fetch_first(pair):
    return [from_behind((pair[0], pair[1]), "seq", distance) for distance in range(REACH, 0, -1)]


def fetch_later(values_b):
    return [from_behind(values_b, "seq", distance) for distance in range(REACH, 0, -1)]


def local(state_in, query_vectors, key_vectors, value_weight, out_weight, doc_ids, cotangent):
    rows_here = state_in.shape[0]
    blocks_here = rows_here // BLOCK
    width_here = query_vectors.shape[1]
    heads_here = width_here // HEAD_DIM
    window_rows = (REACH + 1) * rows_here
    pad_rows = REACH * rows_here
    device_index = lax.axis_index("seq")
    score_scale = 1.0 / math.sqrt(HEAD_DIM)
    doc_padded = jnp.concatenate([jnp.full((REACH * blocks_here,), -1, jnp.int32), doc_ids])
    window_docs = lax.dynamic_slice_in_dim(
        doc_padded, device_index * blocks_here, (REACH + 1) * blocks_here, 0
    )
    key_docs = jnp.broadcast_to(window_docs[:, None], ((REACH + 1) * blocks_here, BLOCK)).reshape(
        -1
    )
    query_docs = key_docs[pad_rows:]
    slot_rows = jnp.arange(window_rows)
    query_rows = jnp.arange(rows_here) + pad_rows
    allowed = (key_docs[None, :] == query_docs[:, None]) & (
        slot_rows[None, :] <= query_rows[:, None]
    )
    gathered_value, gathered_out = in_one_piece((value_weight, out_weight), "seq", 1, 0)
    value_rows = gathered_value[0]
    out_rows = gathered_out[0]
    current = state_in.astype(jnp.float32)
    records = []
    soft_weights = None
    for unroll_step in range(UNROLL):
        normed, inverse_rms = normalize(current)
        values_b = contract_last(normed.astype(jnp.bfloat16), value_rows).astype(jnp.bfloat16)
        if unroll_step == 0:
            received = fetch_first((key_vectors, values_b))
            window_keys = jnp.concatenate([pair[0] for pair in received] + [key_vectors], 0)
            window_values = jnp.concatenate([pair[1] for pair in received] + [values_b], 0)
            query_heads = query_vectors.reshape(rows_here, heads_here, HEAD_DIM)
            key_heads = window_keys.reshape(window_rows, heads_here, HEAD_DIM)
            scores = (
                jnp.einsum(
                    "qhd,khd->hqk", query_heads, key_heads, preferred_element_type=jnp.float32
                )
                * score_scale
            )
            masked = jnp.where(allowed[None], scores, -1e30)
            maxima = jnp.max(masked, axis=2, keepdims=True)
            raised = jnp.where(allowed[None], jnp.exp(masked - maxima), 0.0)
            denominator = jnp.sum(raised, axis=2, keepdims=True)
            soft_weights = (raised / denominator).astype(jnp.bfloat16)
        else:
            received = fetch_later(values_b)
            window_values = jnp.concatenate(received + [values_b], 0)
        attended = jnp.einsum(
            "hqk,khd->qhd",
            soft_weights,
            window_values.reshape(window_rows, heads_here, HEAD_DIM),
            preferred_element_type=jnp.float32,
        )
        attended = attended.reshape(rows_here, width_here).astype(jnp.bfloat16)
        current = current + head_total(
            jnp.dot(attended, out_rows, preferred_element_type=jnp.float32)
        )
        records.append((normed, inverse_rms))
    final_state = current.astype(jnp.bfloat16)
    gradient = cotangent.astype(jnp.float32)
    for normed, inverse_rms in reversed(records):
        grad_b = gradient.astype(jnp.bfloat16)
        d_attended = contract_last(grad_b, out_rows).astype(jnp.bfloat16)
        slot_terms = jnp.einsum(
            "hqk,qhd->khd",
            soft_weights,
            d_attended.reshape(rows_here, heads_here, HEAD_DIM),
            preferred_element_type=jnp.float32,
        )
        slot_terms = slot_terms.reshape(REACH + 1, rows_here, width_here).astype(jnp.bfloat16)
        returned = [
            from_behind(slot_terms[REACH - distance], "seq", -distance)
            for distance in range(1, REACH + 1)
        ]
        running = slot_terms[REACH].astype(jnp.float32)
        for piece_back in returned:
            running = running + piece_back.astype(jnp.float32)
        dvalues = running.astype(jnp.bfloat16)
        d_normed = head_total(jnp.dot(dvalues, value_rows, preferred_element_type=jnp.float32))
        gradient = gradient + inverse_rms * (
            d_normed - normed * jnp.mean(d_normed * normed, axis=-1, keepdims=True)
        )
    return (final_state, gradient)


def solution(mesh):
    placed = (
        P("seq", None),
        P("seq", "fsdp"),
        P("seq", "fsdp"),
        P("fsdp", "seq", None),
        P("fsdp", "seq", None),
        P(),
        P("seq", None),
    )
    return jax.shard_map(
        local,
        mesh=mesh,
        in_specs=placed,
        out_specs=(P("seq", None), P("seq", None)),
        check_vma=False,
    )
```

profile of v0, /device:TPU:14, one launch (start us, length us, event | category | flops | bytes accessed | tf_op | source)
XLA Modules:
  0.0 578.2 jit_solution(5686660754358369850)
XLA Ops:
  11.8 5.8 %collective-permute-start.4 = (bf16[128,1344]{0,1:T(8,128)(2,1)S(1)}, bf16[128,1344]{0,1:T(8,128)(2,1)S(1)}, u32[]{:S(2)}, u32[]{:S(2)}) collective-permute-start(bf16[128,1344]{0,1:T(8,128)(2,1)S(1)} %copy-done.20), channel_id=1, source_target_pairs={{0,8},{2,10},{4,12},{6,14},{8,16},{10,18},{12,20},{14,22},{16,24},... | collective-permute-start | bytes 1032200 | tf_op jit(solution)/shard_map/ppermute | solution.py:30
  19.7 2.8 collective-permute-start.6
  27.2 7.3 %collective-permute-done.5 = bf16[128,1344]{0,1:T(8,128)(2,1)S(1)} collective-permute-done((bf16[128,1344]{0,1:T(8,128)(2,1)S(1)}, bf16[128,1344]{0,1:T(8,128)(2,1)S(1)}, u32[]{:S(2)}, u32[]{:S(2)}) %collective-permute-start.5) | collective-permute-done | bytes 344096 | tf_op jit(solution)/shard_map/ppermute | solution.py:30
  34.6 24.1 %collective-permute-done.6 = bf16[128,1344]{0,1:T(8,128)(2,1)S(1)} collective-permute-done((bf16[128,1344]{0,1:T(8,128)(2,1)S(1)}, bf16[128,1344]{0,1:T(8,128)(2,1)S(1)}, u32[]{:S(2)}, u32[]{:S(2)}) %collective-permute-start.6) | collective-permute-done | bytes 344096 | tf_op jit(solution)/shard_map/ppermute | solution.py:30
  58.8 7.6 %collective-permute-done.7 = bf16[128,1344]{0,1:T(8,128)(2,1)S(1)} collective-permute-done((bf16[128,1344]{0,1:T(8,128)(2,1)S(1)}, bf16[128,1344]{0,1:T(8,128)(2,1)S(1)}, u32[]{:S(2)}, u32[]{:S(2)}) %collective-permute-start.7) | collective-permute-done | bytes 344096 | tf_op jit(solution)/shard_map/ppermute | solution.py:30
  67.7 5.6 fusion.37
  73.4 2.9 divide_convert_fusion
  76.3 114.8 %all-gather.2.cloned.1.call-done = bf16[2,1344,5280]{2,0,1:T(2,128)(2,1)} async-done(((bf16[2,21,5280]{2,0,1:T(2,128)(2,1)}), bf16[2,1344,5280]{2,0,1:T(2,128)(2,1)}) %all-gather.2.cloned.1.call-update) | async-done | bytes 28385296 | tf_op jit(solution)/shard_map/all_gather | solution.py:39
  191.1 53.7 %fusion.34 = (bf16[1,1344,5280]{2,0,1:T(2,128)(2,1)}, bf16[1,1344,5280]{2,0,1:T(2,128)(2,1)}) fusion(bf16[2,1344,5280]{2,0,1:T(2,128)(2,1)} %all-gather.2.cloned.1.call-done), kind=kLoop, calls=%fused_computation.86 | loop fusion | bytes 56770560 | tf_op jit(solution)/shard_map/split | solution.py:39
  244.8 13.9 %copy.40 = bf16[1,1344,5280]{2,1,0:T(8,128)(2,1)S(1)} copy(bf16[1,1344,5280]{2,0,1:T(2,128)(2,1)} %get-tuple-element.3) | data formatting | bytes 28385280
  258.7 4.0 convolution_convert_fusion.6
  263.8 5.3 collective-permute-start
  269.1 5.7 collective-permute-start.1
  274.8 2.8 collective-permute-start.2
  279.6 13.9 %copy.39 = bf16[1,1344,5280]{2,1,0:T(8,128)(2,1)S(1)} copy(bf16[1,1344,5280]{2,0,1:T(2,128)(2,1)} %get-tuple-element.2) | data formatting | bytes 28385280
  293.5 4.0 convolution_convert_fusion.7
  302.1 9.7 %convolution_convert_fusion.3 = bf16[128,5280]{0,1:T(8,128)(2,1)S(1)} fusion(bf16[128,1344]{0,1:T(8,128)(2,1)S(1)} %bitcast.90, bf16[1344,5280]{1,0:T(8,128)(2,1)} %bitcast.75), kind=kOutput, calls=%fused_computation.6 | convolution fusion | flops 1817333760 | bytes 15888384 | tf_op jit(solution)/shard_map/dot_general | solution.py:125
  313.5 3.9 all-to-all-start
  318.9 5.8 collective-permute-start.12
  324.7 3.5 collective-permute-start.13
  330.1 4.0 collective-permute-start.15
  334.2 13.2 %collective-permute-done.13 = bf16[128,1344]{0,1:T(8,128)(2,1)S(1)} collective-permute-done((bf16[128,1344]{0,1:T(8,128)(2,1)S(1)}, bf16[128,1344]{0,1:T(8,128)(2,1)S(1)}, u32[]{:S(2)}, u32[]{:S(2)}) %collective-permute-start.13) | collective-permute-done | bytes 344096 | tf_op jit(solution)/shard_map/ppermute | solution.py:30
  347.4 7.7 %collective-permute-done.14 = bf16[128,1344]{0,1:T(8,128)(2,1)S(1)} collective-permute-done((bf16[128,1344]{0,1:T(8,128)(2,1)S(1)}, bf16[128,1344]{0,1:T(8,128)(2,1)S(1)}, u32[]{:S(2)}, u32[]{:S(2)}) %collective-permute-start.14) | collective-permute-done | bytes 344096 | tf_op jit(solution)/shard_map/ppermute | solution.py:30
  355.1 5.0 collective-permute-done.15
  360.1 10.8 %convolution_convert_fusion.1 = bf16[128,5280]{0,1:T(8,128)(2,1)} fusion(bf16[1344,5280]{1,0:T(8,128)(2,1)} %bitcast.79, bf16[128,1344]{0,1:T(8,128)(2,1)S(1)} %bitcast.88, bf16[128,1344]{0,1:T(8,128)(2,1)S(1)} %collective-permute-done.15, bf16[128,1344]{0,1:T(8,128)(2,1)S(1)} %collective-permute-done.14, bf16[128,1344]{0,1:T(8,128)(2,1)S(1)} %collective-permute-done.13, ...), kind=kOutput, calls=%fused_computation.4 | convolution fusion | flops 1819054080 | bytes 17264640 | tf_op jit(solution)/shard_map/dot_general | solution.py:148
  370.9 5.6 all-to-all-done
  376.6 4.2 broadcast_in_dim.34
  380.7 5.1 all-to-all-start.2
  385.8 2.6 convert_reduce_fusion.3
  389.2 29.3 %all-to-all-done.2 = bf16[2,128,5280]{1,2,0:T(8,128)(2,1)} async-done(((bf16[2,128,5280]{1,2,0:T(8,128)(2,1)}), bf16[2,128,5280]{1,2,0:T(8,128)(2,1)}, u32[]{:S(2)}, u32[]{:S(2)}) %all-to-all-start.2) | async-done | bytes 2703392 | tf_op jit(solution)/shard_map/all_to_all | solution.py:19
  418.5 2.7 convert_reduce_fusion.1
  423.5 7.8 %convolution_convert_fusion.4 = bf16[128,1344]{0,1:T(8,128)(2,1)S(1)} fusion(bf16[1344,5280]{1,0:T(8,128)(2,1)} %bitcast.76, f32[128,5280]{0,1:T(8,128)S(1)} %convert_reduce_fusion.1, bf16[128,5280]{0,1:T(8,128)(2,1)S(1)} %copy-done.18, f32[128]{0:T(128)S(1)} %broadcast_multiply_fusion.1, f32[128]{0:T(128)S(1)} %add_rsqrt_fusion, ...), kind=kOutput, calls=%fused_computation.30 | convolution fusion | flops 1822912512 | bytes 22647808 | tf_op jit(solution)/shard_map/dot_general | solution.py:53
  440.5 4.0 convolution_convert_fusion.5
  444.6 5.4 collective-permute-start.8
  450.0 3.2 collective-permute-start.9
  453.2 3.4 collective-permute-done.17
  458.5 5.9 %collective-permute-done.18 = bf16[128,1344]{0,1:T(8,128)(2,1)S(1)} collective-permute-done((bf16[128,1344]{0,1:T(8,128)(2,1)S(1)}, bf16[128,1344]{0,1:T(8,128)(2,1)S(1)}, u32[]{:S(2)}, u32[]{:S(2)}) %collective-permute-start.18) | collective-permute-done | bytes 344096 | tf_op jit(solution)/shard_map/ppermute | solution.py:30
  466.4 3.5 collective-permute-done.19
  469.9 9.8 %convolution_convert_fusion = bf16[128,5280]{0,1:T(8,128)(2,1)S(1)} fusion(bf16[1344,5280]{1,0:T(8,128)(2,1)} %bitcast.80, bf16[128,1344]{0,1:T(8,128)(2,1)S(1)} %bitcast.87, bf16[128,1344]{0,1:T(8,128)(2,1)S(1)} %collective-permute-done.19, bf16[128,1344]{0,1:T(8,128)(2,1)S(1)} %collective-permute-done.18, ...), kind=kOutput, calls=%fused_computation.3 | convolution fusion | flops 1819054080 | bytes 17264640 | tf_op jit(solution)/shard_map/dot_general | solution.py:148
  481.3 5.3 all-to-all-start.3
  491.9 10.8 %convolution_convert_fusion.2 = bf16[128,5280]{0,1:T(8,128)(2,1)} fusion(bf16[128,1344]{0,1:T(8,128)(2,1)S(1)} %bitcast.89, bf16[1344,5280]{1,0:T(8,128)(2,1)} %bitcast.77), kind=kOutput, calls=%fused_computation.5 | convolution fusion | flops 1817333760 | bytes 15888384 | tf_op jit(solution)/shard_map/dot_general | solution.py:125
  502.6 17.6 %all-to-all-done.3 = bf16[2,128,5280]{1,2,0:T(8,128)(2,1)} async-done(((bf16[2,128,5280]{1,2,0:T(8,128)(2,1)}), bf16[2,128,5280]{1,2,0:T(8,128)(2,1)}, u32[]{:S(2)}, u32[]{:S(2)}) %all-to-all-start.3) | async-done | bytes 2703392 | tf_op jit(solution)/shard_map/all_to_all | solution.py:19
  520.3 3.2 broadcast_in_dim.33
  523.5 5.1 all-to-all-start.1
  528.6 2.6 convert_reduce_fusion
  532.7 29.7 %all-to-all-done.1 = bf16[2,128,5280]{1,2,0:T(8,128)(2,1)} async-done(((bf16[2,128,5280]{1,2,0:T(8,128)(2,1)}), bf16[2,128,5280]{1,2,0:T(8,128)(2,1)}, u32[]{:S(2)}, u32[]{:S(2)}) %all-to-all-start.1) | async-done | bytes 2703392 | tf_op jit(solution)/shard_map/all_to_all | solution.py:19
  562.4 2.7 convert_reduce_fusion.2
  565.8 5.1 fusion.8
  (118 shorter events, 50.6 us)
Async XLA Ops:
  7.2 60.6 %copy-start = (bf16[128,1344]{0,1:T(8,128)(2,1)S(1)}, bf16[128,1344]{0,1:T(8,128)(2,1)}, u32[]{:S(2)}) copy-start(bf16[128,1344]{0,1:T(8,128)(2,1)} %param.8) | copy-start | bytes 1032196
  7.2 4.6 copy-start.20
  7.2 17.2 %copy-start.22 = (s32[64]{0:T(128)S(1)}, s32[64]{0:T(128)}, u32[]{:S(2)}) copy-start(s32[64]{0:T(128)} %param.12) | copy-start | bytes 772
  7.2 18.9 %copy-start.7 = (bf16[128,5280]{0,1:T(8,128)(2,1)S(1)}, bf16[128,5280]{0,1:T(8,128)(2,1)}, u32[]{:S(2)}) copy-start(bf16[128,5280]{0,1:T(8,128)(2,1)} %param.7) | copy-start | bytes 4055044
  7.2 183.9 %all-gather.2.cloned.1.call-start = ((), (), s32[]{:S(2)}) async-start(), calls=%async_computation.4 | async-start | bytes 29352960 | tf_op jit(solution)/shard_map/all_gather | solution.py:39
  11.8 15.3 %collective-permute-start.4 = (bf16[128,1344]{0,1:T(8,128)(2,1)S(1)}, bf16[128,1344]{0,1:T(8,128)(2,1)S(1)}, u32[]{:S(2)}, u32[]{:S(2)}) collective-permute-start(bf16[128,1344]{0,1:T(8,128)(2,1)S(1)} %copy-done.20), channel_id=1, source_target_pairs={{0,8},{2,10},{4,12},{6,14},{8,16},{10,18},{12,20},{14,22},{16,24},... | collective-permute-start | bytes 1032200 | tf_op jit(solution)/shard_map/ppermute | solution.py:30
  17.6 16.9 %collective-permute-start.5 = (bf16[128,1344]{0,1:T(8,128)(2,1)S(1)}, bf16[128,1344]{0,1:T(8,128)(2,1)S(1)}, u32[]{:S(2)}, u32[]{:S(2)}) collective-permute-start(bf16[128,1344]{0,1:T(8,128)(2,1)S(1)} %copy-done.20), channel_id=1, source_target_pairs={{0,6},{2,8},{4,10},{6,12},{8,14},{10,16},{12,18},{14,20},{16,22},{... | collective-permute-start | bytes 1032200 | tf_op jit(solution)/shard_map/ppermute | solution.py:30
  19.7 39.0 %collective-permute-start.6 = (bf16[128,1344]{0,1:T(8,128)(2,1)S(1)}, bf16[128,1344]{0,1:T(8,128)(2,1)S(1)}, u32[]{:S(2)}, u32[]{:S(2)}) collective-permute-start(bf16[128,1344]{0,1:T(8,128)(2,1)S(1)} %copy-done.20), channel_id=1, source_target_pairs={{0,4},{2,6},{4,8},{6,10},{8,12},{10,14},{12,16},{14,18},{16,20},{1... | collective-permute-start | bytes 1032200 | tf_op jit(solution)/shard_map/ppermute | solution.py:30
  22.5 43.9 %collective-permute-start.7 = (bf16[128,1344]{0,1:T(8,128)(2,1)S(1)}, bf16[128,1344]{0,1:T(8,128)(2,1)S(1)}, u32[]{:S(2)}, u32[]{:S(2)}) collective-permute-start(bf16[128,1344]{0,1:T(8,128)(2,1)S(1)} %copy-done.20), channel_id=1, source_target_pairs={{0,2},{2,4},{4,6},{6,8},{8,10},{10,12},{12,14},{14,16},{16,18},{18... | collective-permute-start | bytes 1032200 | tf_op jit(solution)/shard_map/ppermute | solution.py:30
  76.3 225.0 %copy-start.4 = (bf16[14,128,640]{1,2,0:T(8,128)(2,1)}, bf16[14,128,640]{1,2,0:T(8,128)(2,1)S(1)}, u32[]{:S(2)}) copy-start(bf16[14,128,640]{1,2,0:T(8,128)(2,1)S(1)} %divide_convert_fusion) | copy-start | bytes 6881284
  244.8 13.9 %copy-start.8 = (bf16[128,5280]{0,1:T(8,128)(2,1)S(1)}, bf16[128,5280]{0,1:T(8,128)(2,1)}, u32[]{:S(2)}) copy-start(bf16[128,5280]{0,1:T(8,128)(2,1)} %param.7) | copy-start | bytes 4055044
  258.7 5.1 copy-start.3
  263.8 37.1 %collective-permute-start = (bf16[128,1344]{0,1:T(8,128)(2,1)S(1)}, bf16[128,1344]{0,1:T(8,128)(2,1)S(1)}, u32[]{:S(2)}, u32[]{:S(2)}) collective-permute-start(bf16[128,1344]{0,1:T(8,128)(2,1)S(1)} %convolution_convert_fusion.6), channel_id=1, source_target_pairs={{0,8},{2,10},{4,12},{6,14},{8,16},{10,18},{12,20},{14,22},{16,24},... | collective-permute-start | bytes 1032200 | tf_op jit(solution)/shard_map/ppermute | solution.py:30
  269.1 31.8 %collective-permute-start.1 = (bf16[128,1344]{0,1:T(8,128)(2,1)S(1)}, bf16[128,1344]{0,1:T(8,128)(2,1)S(1)}, u32[]{:S(2)}, u32[]{:S(2)}) collective-permute-start(bf16[128,1344]{0,1:T(8,128)(2,1)S(1)} %convolution_convert_fusion.6), channel_id=1, source_target_pairs={{0,6},{2,8},{4,10},{6,12},{8,14},{10,16},{12,18},{14,20},{16,22},{... | collective-permute-start | bytes 1032200 | tf_op jit(solution)/shard_map/ppermute | solution.py:30
  274.8 26.2 %collective-permute-start.2 = (bf16[128,1344]{0,1:T(8,128)(2,1)S(1)}, bf16[128,1344]{0,1:T(8,128)(2,1)S(1)}, u32[]{:S(2)}, u32[]{:S(2)}) collective-permute-start(bf16[128,1344]{0,1:T(8,128)(2,1)S(1)} %convolution_convert_fusion.6), channel_id=1, source_target_pairs={{0,4},{2,6},{4,8},{6,10},{8,12},{10,14},{12,16},{14,18},{16,20},{1... | collective-permute-start | bytes 1032200 | tf_op jit(solution)/shard_map/ppermute | solution.py:30
  277.7 23.5 %collective-permute-start.3 = (bf16[128,1344]{0,1:T(8,128)(2,1)S(1)}, bf16[128,1344]{0,1:T(8,128)(2,1)S(1)}, u32[]{:S(2)}, u32[]{:S(2)}) collective-permute-start(bf16[128,1344]{0,1:T(8,128)(2,1)S(1)} %convolution_convert_fusion.6), channel_id=1, source_target_pairs={{0,2},{2,4},{4,6},{6,8},{8,10},{10,12},{12,14},{14,16},{16,18},{18... | collective-permute-start | bytes 1032200 | tf_op jit(solution)/shard_map/ppermute | solution.py:30
  279.6 13.9 %copy-start.17 = (bf16[128,5280]{0,1:T(8,128)(2,1)S(1)}, bf16[128,5280]{0,1:T(8,128)(2,1)}, u32[]{:S(2)}) copy-start(bf16[128,5280]{0,1:T(8,128)(2,1)} %param.13) | copy-start | bytes 4055044
  293.5 5.2 copy-start.2
  313.5 63.1 %all-to-all-start = ((bf16[2,128,5280]{1,2,0:T(8,128)(2,1)}), bf16[2,128,5280]{1,2,0:T(8,128)(2,1)S(1)}, u32[]{:S(2)}, u32[]{:S(2)}) async-start(bf16[2,128,5280]{1,2,0:T(8,128)(2,1)} %broadcast_in_dim.32), calls=%async_computation | async-start | bytes 5406720 | tf_op jit(solution)/shard_map/all_to_all | solution.py:19
  318.9 15.2 %collective-permute-start.12 = (bf16[128,1344]{0,1:T(8,128)(2,1)S(1)}, bf16[128,1344]{0,1:T(8,128)(2,1)S(1)}, u32[]{:S(2)}, u32[]{:S(2)}) collective-permute-start(bf16[128,1344]{0,1:T(8,128)(2,1)S(1)} %bitcast.98), channel_id=1, source_target_pairs={{2,0},{4,2},{6,4},{8,6},{10,8},{12,10},{14,12},{16,14},{18,16},{20... | collective-permute-start | bytes 1032200 | tf_op jit(solution)/shard_map/ppermute | solution.py:30
  324.7 22.7 %collective-permute-start.13 = (bf16[128,1344]{0,1:T(8,128)(2,1)S(1)}, bf16[128,1344]{0,1:T(8,128)(2,1)S(1)}, u32[]{:S(2)}, u32[]{:S(2)}) collective-permute-start(bf16[128,1344]{0,1:T(8,128)(2,1)S(1)} %bitcast.97), channel_id=1, source_target_pairs={{4,0},{6,2},{8,4},{10,6},{12,8},{14,10},{16,12},{18,14},{20,16},{2... | collective-permute-start | bytes 1032200 | tf_op jit(solution)/shard_map/ppermute | solution.py:30
  328.2 26.9 %collective-permute-start.14 = (bf16[128,1344]{0,1:T(8,128)(2,1)S(1)}, bf16[128,1344]{0,1:T(8,128)(2,1)S(1)}, u32[]{:S(2)}, u32[]{:S(2)}) collective-permute-start(bf16[128,1344]{0,1:T(8,128)(2,1)S(1)} %bitcast.95), channel_id=1, source_target_pairs={{6,0},{8,2},{10,4},{12,6},{14,8},{16,10},{18,12},{20,14},{22,16},{... | collective-permute-start | bytes 1032200 | tf_op jit(solution)/shard_map/ppermute | solution.py:30
  330.1 30.0 %collective-permute-start.15 = (bf16[128,1344]{0,1:T(8,128)(2,1)S(1)}, bf16[128,1344]{0,1:T(8,128)(2,1)S(1)}, u32[]{:S(2)}, u32[]{:S(2)}) collective-permute-start(bf16[128,1344]{0,1:T(8,128)(2,1)S(1)} %bitcast.94), channel_id=1, source_target_pairs={{8,0},{10,2},{12,4},{14,6},{16,8},{18,10},{20,12},{22,14},{24,16},... | collective-permute-start | bytes 1032200 | tf_op jit(solution)/shard_map/ppermute | solution.py:30
  376.5 4.2 copy-start.16
  380.7 37.7 %all-to-all-start.2 = ((bf16[2,128,5280]{1,2,0:T(8,128)(2,1)}), bf16[2,128,5280]{1,2,0:T(8,128)(2,1)}, u32[]{:S(2)}, u32[]{:S(2)}) async-start(bf16[2,128,5280]{1,2,0:T(8,128)(2,1)} %broadcast_in_dim.34), calls=%async_computation.2 | async-start | bytes 5406720 | tf_op jit(solution)/shard_map/all_to_all | solution.py:19
  385.8 2.6 copy-start.9
  418.5 2.7 copy-start.10
  421.2 19.3 %slice-start = ((s8[14450688]{0:T(1024)(128)(4,1)}), s8[4194304]{0:T(1024)(128)(4,1)S(1)}, s32[]{:S(2)}) async-start(s8[14450688]{0:T(1024)(128)(4,1)} %bitcast.81), calls=%async_computation.5 | async-start | bytes 8388608
  423.5 7.8 %copy-start.5 = (bf16[14,128,640]{1,2,0:T(8,128)(2,1)S(1)}, bf16[14,128,640]{1,2,0:T(8,128)(2,1)}, u32[]{:S(2)}) copy-start(bf16[14,128,640]{1,2,0:T(8,128)(2,1)} %copy-done.4) | copy-start | bytes 6881284
  423.5 17.0 %slice-start.1 = ((s8[14450688]{0:T(1024)(128)(4,1)}), s8[4194304]{0:T(1024)(128)(4,1)S(1)}, s32[]{:S(2)}) async-start(s8[14450688]{0:T(1024)(128)(4,1)} %bitcast.81), calls=%async_computation.6 | async-start | bytes 8388608
  423.5 17.0 %slice-start.2 = ((s8[14450688]{0:T(1024)(128)(4,1)}), s8[4194304]{0:T(1024)(128)(4,1)S(1)}, s32[]{:S(2)}) async-start(s8[14450688]{0:T(1024)(128)(4,1)} %bitcast.81), calls=%async_computation.7 | async-start | bytes 8388608
  423.5 17.0 %slice-start.3 = ((s8[14450688]{0:T(1024)(128)(4,1)}), s8[1867776]{0:T(1024)(128)(4,1)S(1)}, s32[]{:S(2)}) async-start(s8[14450688]{0:T(1024)(128)(4,1)} %bitcast.81), calls=%async_computation.8 | async-start | bytes 3735552
  432.6 17.4 %collective-permute-start.16 = (bf16[128,1344]{0,1:T(8,128)(2,1)S(1)}, bf16[128,1344]{0,1:T(8,128)(2,1)S(1)}, u32[]{:S(2)}, u32[]{:S(2)}) collective-permute-start(bf16[128,1344]{0,1:T(8,128)(2,1)S(1)} %bitcast.96), channel_id=1, source_target_pairs={{2,0},{4,2},{6,4},{8,6},{10,8},{12,10},{14,12},{16,14},{18,16},{20... | collective-permute-start | bytes 1032200 | tf_op jit(solution)/shard_map/ppermute | solution.py:30
  434.5 22.1 %collective-permute-start.17 = (bf16[128,1344]{0,1:T(8,128)(2,1)S(1)}, bf16[128,1344]{0,1:T(8,128)(2,1)S(1)}, u32[]{:S(2)}, u32[]{:S(2)}) collective-permute-start(bf16[128,1344]{0,1:T(8,128)(2,1)S(1)} %bitcast.93), channel_id=1, source_target_pairs={{4,0},{6,2},{8,4},{10,6},{12,8},{14,10},{16,12},{18,14},{20,16},{2... | collective-permute-start | bytes 1032200 | tf_op jit(solution)/shard_map/ppermute | solution.py:30
  436.4 28.0 %collective-permute-start.18 = (bf16[128,1344]{0,1:T(8,128)(2,1)S(1)}, bf16[128,1344]{0,1:T(8,128)(2,1)S(1)}, u32[]{:S(2)}, u32[]{:S(2)}) collective-permute-start(bf16[128,1344]{0,1:T(8,128)(2,1)S(1)} %bitcast.92), channel_id=1, source_target_pairs={{6,0},{8,2},{10,4},{12,6},{14,8},{16,10},{18,12},{20,14},{22,16},{... | collective-permute-start | bytes 1032200 | tf_op jit(solution)/shard_map/ppermute | solution.py:30
  438.4 31.5 %collective-permute-start.19 = (bf16[128,1344]{0,1:T(8,128)(2,1)S(1)}, bf16[128,1344]{0,1:T(8,128)(2,1)S(1)}, u32[]{:S(2)}, u32[]{:S(2)}) collective-permute-start(bf16[128,1344]{0,1:T(8,128)(2,1)S(1)} %bitcast.91), channel_id=1, source_target_pairs={{8,0},{10,2},{12,4},{14,6},{16,8},{18,10},{20,12},{22,14},{24,16},... | collective-permute-start | bytes 1032200 | tf_op jit(solution)/shard_map/ppermute | solution.py:30
  444.6 42.1 %collective-permute-start.8 = (bf16[128,1344]{0,1:T(8,128)(2,1)S(1)}, bf16[128,1344]{0,1:T(8,128)(2,1)}, u32[]{:S(2)}, u32[]{:S(2)}) collective-permute-start(bf16[128,1344]{0,1:T(8,128)(2,1)S(1)} %convolution_convert_fusion.5), channel_id=1, source_target_pairs={{0,8},{2,10},{4,12},{6,14},{8,16},{10,18},{12,20},{14,22},{16,24},... | collective-permute-start | bytes 1032200 | tf_op jit(solution)/shard_map/ppermute | solution.py:30
  450.0 37.9 %collective-permute-start.9 = (bf16[128,1344]{0,1:T(8,128)(2,1)S(1)}, bf16[128,1344]{0,1:T(8,128)(2,1)}, u32[]{:S(2)}, u32[]{:S(2)}) collective-permute-start(bf16[128,1344]{0,1:T(8,128)(2,1)S(1)} %convolution_convert_fusion.5), channel_id=1, source_target_pairs={{0,6},{2,8},{4,10},{6,12},{8,14},{10,16},{12,18},{14,20},{16,22},{... | collective-permute-start | bytes 1032200 | tf_op jit(solution)/shard_map/ppermute | solution.py:30
  456.6 32.3 %collective-permute-start.10 = (bf16[128,1344]{0,1:T(8,128)(2,1)S(1)}, bf16[128,1344]{0,1:T(8,128)(2,1)}, u32[]{:S(2)}, u32[]{:S(2)}) collective-permute-start(bf16[128,1344]{0,1:T(8,128)(2,1)S(1)} %convolution_convert_fusion.5), channel_id=1, source_target_pairs={{0,4},{2,6},{4,8},{6,10},{8,12},{10,14},{12,16},{14,18},{16,20},{1... | collective-permute-start | bytes 1032200 | tf_op jit(solution)/shard_map/ppermute | solution.py:30
  464.5 25.6 %collective-permute-start.11 = (bf16[128,1344]{0,1:T(8,128)(2,1)S(1)}, bf16[128,1344]{0,1:T(8,128)(2,1)}, u32[]{:S(2)}, u32[]{:S(2)}) collective-permute-start(bf16[128,1344]{0,1:T(8,128)(2,1)S(1)} %convolution_convert_fusion.5), channel_id=1, source_target_pairs={{0,2},{2,4},{4,6},{6,8},{8,10},{10,12},{12,14},{14,16},{16,18},{18... | collective-permute-start | bytes 1032200 | tf_op jit(solution)/shard_map/ppermute | solution.py:30
  481.3 38.9 %all-to-all-start.3 = ((bf16[2,128,5280]{1,2,0:T(8,128)(2,1)}), bf16[2,128,5280]{1,2,0:T(8,128)(2,1)}, u32[]{:S(2)}, u32[]{:S(2)}) async-start(bf16[2,128,5280]{1,2,0:T(8,128)(2,1)} %broadcast_in_dim.35), calls=%async_computation.3 | async-start | bytes 5406720 | tf_op jit(solution)/shard_map/all_to_all | solution.py:19
  486.6 4.5 copy-start.6
  523.5 38.9 %all-to-all-start.1 = ((bf16[2,128,5280]{1,2,0:T(8,128)(2,1)}), bf16[2,128,5280]{1,2,0:T(8,128)(2,1)}, u32[]{:S(2)}, u32[]{:S(2)}) async-start(bf16[2,128,5280]{1,2,0:T(8,128)(2,1)} %broadcast_in_dim.33), calls=%async_computation.1 | async-start | bytes 5406720 | tf_op jit(solution)/shard_map/all_to_all | solution.py:19
  528.6 2.6 copy-start.11
  562.4 2.7 copy-start.12
  562.4 3.0 copy-start.14
  562.4 3.4 copy-start.19
  565.8 5.1 copy-start.1
  (4 other events, 6.5 us)
Sparse Core Ops, SparseCore 0:
  11.9 179.0 all-gather.1
where the time goes:
time: 588 us; the launch traced here: 578 us
  waiting for transfers between devices  275 us (47%)
  local copies, waits for them, and re-layouts  109 us (19%)
  starting transfers between devices  83.2 us (14%)
  matrix products  71 us (12%)
  other arithmetic  24.3 us (4%)
  between operations  15.2 us (3%)
    all_gather x1, waiting for transfers between devices, in_one_piece(): lax.all_gather(both, axis, axis=dim, tiled=True)  115 us
    all_to_all x4, waiting for transfers between devices, from_everyone(): lax.all_to_all(jnp.broadcast_to(x[None], (size, *x.shape)), axis, 0, 0, t...  82.2 us
    ppermute x20, waiting for transfers between devices, from_behind(): lax.ppermute(value, axis, [(source, source + steps) for source in range(f...  78.2 us
    ppermute x20, starting transfers between devices, from_behind(): lax.ppermute(value, axis, [(source, source + steps) for source in range(f...  63.8 us
    split x1, local copies, waits for them, and re-layouts, in_one_piece(): jnp.split(lax.all_gather(both, axis, axis=dim, tiled=True), ends, axis=al...  53.7 us
    unnamed x70, local copies, waits for them, and re-layouts  42 us
    dot_general x2, matrix products, local(): jnp.dot(dvalues, value_rows, preferred_element_type=jnp.float32)  20.6 us
    dot_general x2, matrix products, local(): jnp.dot(attended, out_rows, preferred_element_type=jnp.float32)  20.5 us
  transfers between devices with their start and end apart: 25, of which 15 were waited for; matrix products, arithmetic and copies ran while one was open for 14% of the time, Pallas kernels for 0%

commit v1 on v0

v1 whole, which is shorter than its diff:
```python
import math

import jax
import jax.numpy as jnp
from jax import lax
from jax.experimental import pallas as pl
from jax.experimental.pallas import tpu as pltpu
from jax.sharding import Mesh
from jax.sharding import PartitionSpec as P

HEAD_DIM = 96
BLOCK = 128
UNROLL = 2
REACH = 4
EPS = 1e-06

D = 5280
QF = 1320
T = 256
HQ = 672
HEADS_Q = 7
UNIT = 24
NPAD = 768
CHIPS = 32

bf16 = jnp.bfloat16
f32 = jnp.float32
PARAMS = pltpu.CompilerParams(vmem_limit_bytes=56 * 1024 * 1024)
SWAP = [(0, 1), (1, 0)]


def window(h):
    lo = (HEAD_DIM * h) // 128 * 128
    hi = min(-(-(HEAD_DIM * (h + 1)) // 128) * 128, HQ)
    return lo, hi


def head_mask(h, lo, hi):
    lane = lax.broadcasted_iota(jnp.int32, (1, hi - lo), 1) + lo
    return (lane >= HEAD_DIM * h) & (lane < HEAD_DIM * (h + 1))


def dot_t(a, b):
    return lax.dot_general(a, b, (((1,), (1,)), ((), ())), preferred_element_type=f32)


def dot(a, b):
    return jnp.dot(a, b, preferred_element_type=f32)


def project_body(sel, x_ref, g_ref, ss_ref, o_ref, *, stats):
    w = g_ref[...].reshape(NPAD, QF)
    out = dot_t(x_ref[...], w)
    if stats:
        ss = ss_ref[...]
        hi = ss.astype(bf16).astype(f32)
        lo = ss - hi
        lane = lax.broadcasted_iota(jnp.int32, (1, NPAD), 1)
        spot = UNIT * sel[2] + 21
        out = out + jnp.where(lane == spot, hi, 0.0) + jnp.where(lane == spot + 1, lo, 0.0)
    o_ref[0] = out.astype(bf16)


def project(x, g, ss, sel, stats):
    import functools

    return pl.pallas_call(
        functools.partial(project_body, stats=stats),
        out_shape=jax.ShapeDtypeStruct((2, T, NPAD), bf16),
        grid_spec=pltpu.PrefetchScalarGridSpec(
            num_scalar_prefetch=1,
            grid=(2,),
            in_specs=[
                pl.BlockSpec((T, QF), lambda i, s: (0, 0)),
                pl.BlockSpec((16, 1, 48, QF), lambda i, s: (0, s[i], 0, 0)),
                pl.BlockSpec((T, 1), lambda i, s: (0, 0)),
            ],
            out_specs=pl.BlockSpec((1, T, NPAD), lambda i, s: (i, 0, 0)),
        ),
        compiler_params=PARAMS,
        name="project",
    )(sel, x, g, ss)


def settle_body(k_ref, c_ref, f_ref, sel_ref, v_ref, inv_ref):
    v = k_ref[0].astype(f32) + c_ref[0].astype(f32) + f_ref[...].astype(f32)
    lane = lax.broadcasted_iota(jnp.int32, (1, 128), 1)
    spot = lane % UNIT
    mark = ((spot == 21) | (spot == 22)) & (lane < 4 * UNIT)
    ss = jnp.sum(jnp.where(mark, v[:, :128], 0.0), axis=1, keepdims=True)
    inv = lax.rsqrt(ss * (1.0 / D) + EPS)
    v_ref[...] = dot((v * inv).astype(bf16), sel_ref[...]).astype(bf16)
    inv_ref[...] = inv


def settle(kept, from_core, from_f, onehot):
    first = pl.BlockSpec((1, T, NPAD), lambda i: (0, 0, 0))
    return pl.pallas_call(
        settle_body,
        out_shape=(jax.ShapeDtypeStruct((T, HQ), bf16), jax.ShapeDtypeStruct((T, 1), f32)),
        grid=(1,),
        out_specs=(
            pl.BlockSpec((T, HQ), lambda i: (0, 0)),
            pl.BlockSpec((T, 1), lambda i: (0, 0)),
        ),
        in_specs=[
            first,
            first,
            pl.BlockSpec((T, NPAD), lambda i: (0, 0)),
            pl.BlockSpec((NPAD, HQ), lambda i: (0, 0)),
        ],
        compiler_params=PARAMS,
        name="settle",
    )(kept, from_core, from_f, onehot)


def softmax_body(q_ref, k2_ref, k1_ref, k0_ref, qd_ref, kd_ref, p_ref, pt_ref):
    row = lax.broadcasted_iota(jnp.int32, (T, 3 * T), 0)
    col = lax.broadcasted_iota(jnp.int32, (T, 3 * T), 1)
    ok = (qd_ref[...] == kd_ref[...]) & (col <= row + 2 * T)
    scale = 1.0 / math.sqrt(HEAD_DIM)
    for h in range(HEADS_Q):
        lo, hi = window(h)
        q = jnp.where(head_mask(h, lo, hi), q_ref[:, lo:hi].astype(f32), 0.0).astype(bf16)
        s = jnp.concatenate(
            [dot_t(q, k2_ref[:, lo:hi]), dot_t(q, k1_ref[:, lo:hi]), dot_t(q, k0_ref[:, lo:hi])],
            axis=1,
        )
        s = jnp.where(ok, s * scale, -1e30)
        top = jnp.max(s, axis=1, keepdims=True)
        e = jnp.where(ok, jnp.exp(s - top), 0.0)
        p = e / jnp.sum(e, axis=1, keepdims=True)
        p_ref[h] = p.astype(bf16)
        pt_ref[h] = p.T.astype(bf16)


def softmax(q, k2, k1, k0, qdoc, kdoc):
    return pl.pallas_call(
        softmax_body,
        out_shape=(
            jax.ShapeDtypeStruct((HEADS_Q, T, 3 * T), bf16),
            jax.ShapeDtypeStruct((HEADS_Q, 3 * T, T), bf16),
        ),
        compiler_params=PARAMS,
        name="softmax",
    )(q, k2, k1, k0, qdoc, kdoc)


def attend_body(p_ref, v2_ref, v1_ref, v0_ref, sel_ref, o_ref, acc_ref):
    acc_ref[...] = jnp.zeros_like(acc_ref)
    for h in range(HEADS_Q):
        lo, hi = window(h)
        out = (
            dot(p_ref[h, :, :T], v2_ref[:, lo:hi])
            + dot(p_ref[h, :, T : 2 * T], v1_ref[:, lo:hi])
            + dot(p_ref[h, :, 2 * T :], v0_ref[:, lo:hi])
        )
        acc_ref[:, lo:hi] += jnp.where(head_mask(h, lo, hi), out, 0.0)
    o_ref[...] = dot_t(acc_ref[...].astype(bf16), sel_ref[...]).astype(bf16)


def attend(p, v2, v1, v0, onehot):
    return pl.pallas_call(
        attend_body,
        out_shape=jax.ShapeDtypeStruct((T, NPAD), bf16),
        scratch_shapes=[pltpu.VMEM((T, HQ), f32)],
        compiler_params=PARAMS,
        name="attend",
    )(p, v2, v1, v0, onehot)


def spread_body(k_ref, c_ref, f_ref, sel_ref, pt_ref, o2_ref, o1_ref, o0_ref, acc_ref):
    v = k_ref[0].astype(f32) + c_ref[0].astype(f32) + f_ref[...].astype(f32)
    da = dot(v.astype(bf16), sel_ref[...]).astype(bf16)
    acc_ref[...] = jnp.zeros_like(acc_ref)
    for h in range(HEADS_Q):
        lo, hi = window(h)
        out = dot(pt_ref[h], da[:, lo:hi])
        acc_ref[:, lo:hi] += jnp.where(head_mask(h, lo, hi), out, 0.0)
    o2_ref[...] = acc_ref[:T].astype(bf16)
    o1_ref[...] = acc_ref[T : 2 * T].astype(bf16)
    o0_ref[...] = acc_ref[2 * T :].astype(bf16)


def spread(kept, from_core, from_f, onehot, pt):
    first = pl.BlockSpec((1, T, NPAD), lambda i: (0, 0, 0))
    one = jax.ShapeDtypeStruct((T, HQ), bf16)
    return pl.pallas_call(
        spread_body,
        out_shape=(one, one, one),
        grid=(1,),
        out_specs=(pl.BlockSpec((T, HQ), lambda i: (0, 0)),) * 3,
        in_specs=[
            first,
            first,
            pl.BlockSpec((T, NPAD), lambda i: (0, 0)),
            pl.BlockSpec((NPAD, HQ), lambda i: (0, 0)),
            pl.BlockSpec((HEADS_Q, 3 * T, T), lambda i: (0, 0, 0)),
        ],
        scratch_shapes=[pltpu.VMEM((3 * T, HQ), f32)],
        compiler_params=PARAMS,
        name="spread",
    )(kept, from_core, from_f, onehot, pt)


def gather_grad_body(o_ref, r1_ref, r2_ref, v_ref, sel_ref, out_ref):
    dv = o_ref[...].astype(f32) + r1_ref[...].astype(f32) + r2_ref[...].astype(f32)
    dv = dv.astype(bf16)
    m = jnp.sum(dv.astype(f32) * v_ref[...].astype(f32), axis=1, keepdims=True)
    hi = m.astype(bf16).astype(f32)
    lo = m - hi
    lane = lax.broadcasted_iota(jnp.int32, (1, NPAD), 1)
    out = dot_t(dv, sel_ref[...])
    out = out + jnp.where(lane == 21, hi, 0.0) + jnp.where(lane == 22, lo, 0.0)
    out_ref[...] = out.astype(bf16)


def gather_grad(own, r1, r2, values, onehot):
    return pl.pallas_call(
        gather_grad_body,
        out_shape=jax.ShapeDtypeStruct((T, NPAD), bf16),
        compiler_params=PARAMS,
        name="gather_grad",
    )(own, r1, r2, values, onehot)


def half_body(sel, a_ref, b_ref, g_ref, base_ref, o_ref):
    i = pl.program_id(0)
    w = g_ref[...].reshape(NPAD, QF)

    @pl.when(i == 0)
    def _():
        o_ref[...] = base_ref[...] + dot(a_ref[...], w)

    @pl.when(i == 1)
    def _():
        o_ref[...] += dot(b_ref[...], w)


def half(a, b, g, base, sel):
    full = pl.BlockSpec((T, NPAD), lambda i, s: (0, 0))
    wide = pl.BlockSpec((T, QF), lambda i, s: (0, 0))
    return pl.pallas_call(
        half_body,
        out_shape=jax.ShapeDtypeStruct((T, QF), f32),
        grid_spec=pltpu.PrefetchScalarGridSpec(
            num_scalar_prefetch=1,
            grid=(2,),
            in_specs=[
                full,
                full,
                pl.BlockSpec((16, 1, 48, QF), lambda i, s: (0, s[i], 0, 0)),
                wide,
            ],
            out_specs=wide,
        ),
        compiler_params=PARAMS,
        name="half",
    )(sel, a, b, g, base)


def update_body(sel, a_ref, b_ref, g_ref, part_ref, o_ref, x_ref, ss_ref):
    i = pl.program_id(0)
    w = g_ref[...].reshape(NPAD, QF)

    @pl.when(i == 0)
    def _():
        o_ref[...] = part_ref[...] + dot(a_ref[...], w)

    @pl.when(i == 1)
    def _():
        new = o_ref[...] + dot(b_ref[...], w)
        o_ref[...] = new
        x_ref[...] = new.astype(bf16)
        ss_ref[...] = jnp.sum(new * new, axis=1, keepdims=True)


def update(a, b, g, part, sel):
    full = pl.BlockSpec((T, NPAD), lambda i, s: (0, 0))
    wide = pl.BlockSpec((T, QF), lambda i, s: (0, 0))
    return pl.pallas_call(
        update_body,
        out_shape=(
            jax.ShapeDtypeStruct((T, QF), f32),
            jax.ShapeDtypeStruct((T, QF), bf16),
            jax.ShapeDtypeStruct((T, 1), f32),
        ),
        grid_spec=pltpu.PrefetchScalarGridSpec(
            num_scalar_prefetch=1,
            grid=(2,),
            in_specs=[
                full,
                full,
                pl.BlockSpec((16, 1, 48, QF), lambda i, s: (0, s[i], 0, 0)),
                wide,
            ],
            out_specs=(wide, wide, pl.BlockSpec((T, 1), lambda i, s: (0, 0))),
        ),
        compiler_params=PARAMS,
        name="update",
    )(sel, a, b, g, part)


def backstep_body(sel, a_ref, b_ref, c_ref, d_ref, g_ref, part_ref, grad_ref, cur_ref, inv_ref, o_ref, x_ref, acc_ref):
    i = pl.program_id(0)
    w = g_ref[...].reshape(NPAD, QF)

    @pl.when(i == 0)
    def _():
        acc_ref[...] = part_ref[...] + dot(a_ref[...], w)

    @pl.when(i == 1)
    def _():
        d_normed = acc_ref[...] + dot(b_ref[...], w)
        lane = lax.broadcasted_iota(jnp.int32, (1, 128), 1)
        mark = (lane == 21) | (lane == 22)
        m = jnp.zeros((T, 1), f32)
        for r in (a_ref, b_ref, c_ref, d_ref):
            m = m + jnp.sum(jnp.where(mark, r[:, :128].astype(f32), 0.0), axis=1, keepdims=True)
        inv = inv_ref[...]
        new = grad_ref[...] + inv * (d_normed - cur_ref[...] * (inv * m * (1.0 / D)))
        o_ref[...] = new
        x_ref[...] = new.astype(bf16)


def backstep(a, b, c, d, g, part, grad, current, inv, sel):
    full = pl.BlockSpec((T, NPAD), lambda i, s: (0, 0))
    wide = pl.BlockSpec((T, QF), lambda i, s: (0, 0))
    return pl.pallas_call(
        backstep_body,
        out_shape=(jax.ShapeDtypeStruct((T, QF), f32), jax.ShapeDtypeStruct((T, QF), bf16)),
        grid_spec=pltpu.PrefetchScalarGridSpec(
            num_scalar_prefetch=1,
            grid=(2,),
            in_specs=[
                full,
                full,
                full,
                full,
                pl.BlockSpec((16, 1, 48, QF), lambda i, s: (0, s[i], 0, 0)),
                wide,
                wide,
                wide,
                pl.BlockSpec((T, 1), lambda i, s: (0, 0)),
            ],
            out_specs=(wide, wide),
            scratch_shapes=[pltpu.VMEM((T, QF), f32)],
        ),
        compiler_params=PARAMS,
        name="backstep",
    )(sel, a, b, c, d, g, part, grad, current, inv)


def assemble_body(sel, a_ref, b_ref, c_ref, d_ref, o_ref):
    for mine in range(4):

        @pl.when(sel[0] == mine)
        def _(mine=mine):
            f, c = mine // 2, mine % 2
            spots = (2 * f + c, 2 * f + 1 - c, 2 * (1 - f) + c, 2 * (1 - f) + 1 - c)
            for q, r in zip(spots, (a_ref, b_ref, c_ref, d_ref)):
                o_ref[:, q * QF : (q + 1) * QF] = r[...].astype(o_ref.dtype)


def assemble(a, b, c, d, sel, dtype):
    part = pl.BlockSpec((BLOCK, QF), lambda i, s: (0, 0))
    return pl.pallas_call(
        assemble_body,
        out_shape=jax.ShapeDtypeStruct((BLOCK, D), dtype),
        grid_spec=pltpu.PrefetchScalarGridSpec(
            num_scalar_prefetch=1,
            grid=(1,),
            in_specs=[part] * 4,
            out_specs=pl.BlockSpec((BLOCK, D), lambda i, s: (0, 0)),
        ),
        compiler_params=PARAMS,
        name="assemble",
    )(sel, a, b, c, d)


def swap_c(x):
    return lax.ppermute(x, "c", SWAP)


def swap_f(x):
    return lax.ppermute(x, "f", SWAP)


def along(x, steps):
    pairs = [(i, i + steps) for i in range(CHIPS) if 0 <= i + steps < CHIPS]
    return lax.ppermute(x, ("yl", "x", "z"), pairs)


def weight_quarter(w):
    rows = jnp.pad(w[0], ((0, UNIT - w.shape[1]), (0, 0)))
    quarters = rows.reshape(UNIT, 2, 2, QF).transpose(1, 2, 0, 3)
    sent = jnp.broadcast_to(quarters[:, None], (2, 2, 2, UNIT, QF)).reshape(8, UNIT, QF)
    got = lax.all_to_all(sent, ("f", "yl", "c"), 0, 0, tiled=True)
    return got.reshape(4, 2 * UNIT, QF)


def token_quarter(x, f):
    part = lax.dynamic_slice_in_dim(x, f * (2 * QF), 2 * QF, 1)
    part = part.reshape(BLOCK, 2, QF).transpose(1, 0, 2)
    return lax.all_to_all(part, "c", 0, 0, tiled=True).reshape(T, QF)


def head_quarter(x):
    part = x.reshape(BLOCK, 2, HQ).transpose(1, 0, 2)
    return lax.all_to_all(part, "c", 0, 0, tiled=True).reshape(T, HQ)


def own_tokens(x, c):
    mine = lax.dynamic_slice_in_dim(x, c * BLOCK, BLOCK, 0)
    theirs = lax.dynamic_slice_in_dim(x, (1 - c) * BLOCK, BLOCK, 0)
    other = swap_c(theirs)
    far = swap_f(mine)
    far_other = swap_f(other)
    return mine, other, far, far_other


def reduced(x, g, ss, away, here, stats):
    sent = project(x, g, ss, away, stats)
    from_core = swap_c(sent)
    kept = project(x, g, ss, here, stats)
    from_f = swap_f(kept[1] + from_core[1])
    return kept, from_core, from_f


def local(state_in, query_vectors, key_vectors, value_weight, out_weight, doc_ids, cotangent):
    c = lax.axis_index("c")
    f = lax.axis_index("f")
    chip = (lax.axis_index("yl") * 4 + lax.axis_index("x")) * 4 + lax.axis_index("z")
    me = 2 * f + c
    near_f = 2 * f + (1 - c)
    far_c = 2 * (1 - f) + c
    far_d = 2 * (1 - f) + (1 - c)
    here = jnp.stack([me, far_c, me]).astype(jnp.int32)
    away = jnp.stack([near_f, far_d, me]).astype(jnp.int32)
    first = jnp.stack([me, near_f]).astype(jnp.int32)
    second = jnp.stack([far_c, far_d]).astype(jnp.int32)

    value_part = weight_quarter(value_weight)
    values_w = lax.all_gather(value_part, ("x", "z"), axis=0)
    out_part = weight_quarter(out_weight)
    out_w = lax.all_gather(out_part, ("x", "z"), axis=0)

    k_pad = jnp.arange(NPAD)[:, None]
    k_nat = jnp.arange(HQ)[None, :]
    onehot = ((k_pad // UNIT * 21 + k_pad % UNIT == k_nat) & (k_pad % UNIT < 21)).astype(bf16)

    docs = jnp.concatenate([jnp.full((REACH,), -1, jnp.int32), doc_ids])
    docs = lax.dynamic_slice_in_dim(docs, 2 * chip, REACH + 2, 0)
    kdoc = jnp.broadcast_to(docs[:, None], (REACH + 2, BLOCK)).reshape(1, 3 * T)
    qdoc = jnp.broadcast_to(docs[REACH:, None], (2, BLOCK)).reshape(T, 1)
    q = head_quarter(query_vectors)
    k = head_quarter(key_vectors)
    p, pt = softmax(q, along(k, 2), along(k, 1), k, qdoc, kdoc)

    x = token_quarter(state_in, f)
    gb = token_quarter(cotangent, f)
    current = x.astype(f32)
    ss = jnp.sum(current * current, axis=1, keepdims=True)
    records = []
    for _ in range(UNROLL):
        kept, from_core, from_f = reduced(x, values_w, ss, away, here, True)
        values, inv = settle(kept, from_core, from_f, onehot)
        v2, v1 = along(values, 2), along(values, 1)
        a = attend(p, v2, v1, values, onehot)
        a_c = swap_c(a)
        a_f = swap_f(a)
        part = half(a, a_c, out_w, current, first)
        a_d = swap_c(a_f)
        records.append((current, inv, values))
        current, x, ss = update(a_f, a_d, out_w, part, second)
    final_state = assemble(*own_tokens(x, c), me[None].astype(jnp.int32), bf16)
    gradient = gb.astype(f32)
    zero = jnp.zeros((T, QF), f32)
    for cur, inv, values in reversed(records):
        kept, from_core, from_f = reduced(gb, out_w, ss, away, here, False)
        o2, o1, o0 = spread(kept, from_core, from_f, onehot, pt)
        r2, r1 = along(o2, -2), along(o1, -1)
        a = gather_grad(o0, r1, r2, values, onehot)
        a_c = swap_c(a)
        a_f = swap_f(a)
        part = half(a, a_c, values_w, zero, first)
        a_d = swap_c(a_f)
        gradient, gb = backstep(a_f, a_d, a, a_c, values_w, part, gradient, cur, inv, second)
    state_grad = assemble(*own_tokens(gb, c), me[None].astype(jnp.int32), f32)
    return (final_state, state_grad)


def solution(mesh):
    fine = Mesh(mesh.devices.reshape(2, 4, 4, 2, 2), ("yl", "x", "z", "c", "f"))
    seq = ("yl", "x", "z", "c")
    placed = (
        P(seq, None),
        P(seq, "f"),
        P(seq, "f"),
        P("f", seq, None),
        P("f", seq, None),
        P(),
        P(seq, None),
    )
    return jax.shard_map(
        local,
        mesh=fine,
        in_specs=placed,
        out_specs=(P(seq, None), P(seq, None)),
        check_vma=False,
    )
```

time: 588 us -> 558 us (0.949)
  the two profiles are of different devices: /device:TPU:14 before, /device:TPU:32 now
where the time goes in v1:
time: 558 us; the launch traced here: 549 us
  waiting for transfers between devices  202 us (36%)
  Pallas kernels  135 us (24%)
  starting transfers between devices  117 us (21%)
  blocking collectives  36.9 us (7%)
  local copies, waits for them, and re-layouts  30.8 us (6%)
  between operations  14.9 us (3%)
  other arithmetic  11.9 us (2%)
    ppermute x12, waiting for transfers between devices, swap_f(): return lax.ppermute(x, 'f', SWAP)  89.7 us
    ppermute x10, starting transfers between devices, along(): return lax.ppermute(x, ('yl', 'x', 'z'), pairs)  75.5 us
    ppermute x10, waiting for transfers between devices, along(): return lax.ppermute(x, ('yl', 'x', 'z'), pairs)  61.8 us
    all_gather x1, waiting for transfers between devices, local(): values_w = lax.all_gather(value_part, ('x', 'z'), axis=0)  48.9 us
    pallas_call x8, Pallas kernels, project(): pl.pallas_call(functools.partial(project_body, stats=stats), out_shape=ja...  39.1 us
    ppermute x12, starting transfers between devices, swap_f(): return lax.ppermute(x, 'f', SWAP)  32.4 us
    all_to_all x2, blocking collectives, weight_quarter(): got = lax.all_to_all(sent, ('f', 'yl', 'c'), 0, 0, tiled=True)  28.7 us
    pallas_call x4, Pallas kernels, half(): pl.pallas_call(half_body, out_shape=jax.ShapeDtypeStruct((T, QF), f32), g...  23.7 us
  transfers between devices with their start and end apart: 40, of which 22 were waited for; matrix products, arithmetic and copies ran while one was open for 4% of the time, Pallas kernels for 13%

profile of v1, /device:TPU:32, one launch (start us, length us, event | category | flops | bytes accessed | tf_op | source)
XLA Modules:
  0.0 548.9 jit_solution(10180765695412140031)
XLA Ops:
  8.7 15.0 %all_to_all.30 = bf16[8,24,1320]{2,1,0:T(8,128)(2,1)} all-to-all(bf16[8,24,1320]{2,1,0:T(8,128)(2,1)S(1)} %bitcast.53), channel_id=1, replica_groups=mesh['yl'=2,'x'=4,'z'=4,'c'=2,'f'=2] {'f','yl','c'}, dimensions={0} | all-to-all | bytes 1013760 | tf_op jit(solution)/shard_map/all_to_all | solution.py:398
  24.3 13.6 %all_to_all.31 = bf16[8,24,1320]{2,1,0:T(8,128)(2,1)} all-to-all(bf16[8,24,1320]{2,1,0:T(8,128)(2,1)S(1)} %bitcast.54), channel_id=1, replica_groups=mesh['yl'=2,'x'=4,'z'=4,'c'=2,'f'=2] {'f','yl','c'}, dimensions={0} | all-to-all | bytes 1013760 | tf_op jit(solution)/shard_map/all_to_all | solution.py:398
  38.9 3.5 all-to-all-start.2
  47.0 48.9 %all-gather.3.cloned.1.call-done.g_ref = bf16[16,4,48,1320]{3,2,1,0:T(8,128)(2,1)} async-done(((bf16[1,4,48,1320]{3,2,1,0:T(8,128)(2,1)}), bf16[16,4,48,1320]{3,2,1,0:T(8,128)(2,1)}) %all-gather.3.cloned.1.call-update) | async-done | bytes 8110096 | tf_op jit(solution)/shard_map/all_gather | solution.py:444
  95.9 5.0 project.9
  100.9 4.0 all_to_all.32
  105.1 4.2 collective-permute-start
  112.7 4.9 project.8.k_ref
  123.5 7.6 %collective-permute-done.3.f_ref = bf16[256,768]{1,0:T(8,128)(2,1)S(1)} collective-permute-done((bf16[256,768]{1,0:T(8,128)(2,1)S(1)}, bf16[256,768]{1,0:T(8,128)(2,1)S(1)}, u32[]{:S(2)}, u32[]{:S(2)}) %collective-permute-start.3) | collective-permute-done | bytes 393248 | tf_op jit(solution)/shard_map/ppermute | solution.py:386
  134.8 26.4 %collective-permute-start.4 = (bf16[256,672]{1,0:T(8,128)(2,1)}, bf16[256,672]{1,0:T(8,128)(2,1)S(1)}, u32[]{:S(2)}, u32[]{:S(2)}) collective-permute-start(bf16[256,672]{1,0:T(8,128)(2,1)} %get-tuple-element.23.v0_ref.v_ref), channel_id=1, source_target_pairs={{0,8},{4,12},{8,16},{12,20},{16,24},{20,28},{24,32},{28,36},{32,40... | collective-permute-start | bytes 1032200 | tf_op jit(solution)/shard_map/ppermute | solution.py:391
  170.2 7.1 %softmax.1 = (bf16[7,256,768]{2,1,0:T(8,128)(2,1)}, bf16[7,768,256]{2,1,0:T(8,128)(2,1)}) custom-call(bf16[256,672]{1,0:T(8,128)(2,1)} %bitcast.58, bf16[256,672]{1,0:T(8,128)(2,1)} %copy-done.28, bf16[256,672]{1,0:T(8,128)(2,1)} %copy-done.29, bf16[256,672]{1,0:T(8,128)(2,1)} %bitcast.57, s32[256,1]{1,0:T(8,128)} %copy.28.qd_ref, s32[1,768]{1,0:T(1,128)} %bitcast.64), custom_call_target="tpu_custom_call" | custom-call | tf_op jit(solution)/shard_map/softmax/pallas_call | solution.py:138
  178.7 4.2 collective-permute-done.5.v1_ref
  183.7 4.7 attend.2.a_ref
  192.3 6.6 %collective-permute-done.6.a_ref = bf16[256,768]{1,0:T(8,128)(2,1)S(1)} collective-permute-done((bf16[256,768]{1,0:T(8,128)(2,1)}, bf16[256,768]{1,0:T(8,128)(2,1)S(1)}, u32[]{:S(2)}, u32[]{:S(2)}) %collective-permute-start.6) | collective-permute-done | bytes 393248 | tf_op jit(solution)/shard_map/ppermute | solution.py:386
  201.1 5.9 %half.4.part_ref = f32[256,1320]{1,0:T(8,128)} custom-call(s32[2]{0:T(128)} %pad_add_fusion.1.sel, bf16[256,768]{1,0:T(8,128)(2,1)} %attend.2.a_ref, bf16[256,768]{1,0:T(8,128)(2,1)} %copy-done.19, bf16[16,4,48,1320]{3,2,1,0:T(8,128)(2,1)} %all-gather.5.cloned.1.call-done.g_ref, f32[256,1320]{1,0:T(8,128)} %bitcast_convert_fusion.1.base_ref.cur_ref), custom_call_target="tpu_custom_call" | custom-call | tf_op jit(solution)/shard_map/half/pallas_call | solution.py:243
  207.8 6.3 %update.2 = (f32[256,1320]{1,0:T(8,128)}, bf16[256,1320]{1,0:T(8,128)(2,1)}, f32[256,1]{1,0:T(8,128)}) custom-call(s32[2]{0:T(128)} %pad_add_fusion.sel, bf16[256,768]{1,0:T(8,128)(2,1)} %copy-done.14, bf16[256,768]{1,0:T(8,128)(2,1)} %copy-done.17, bf16[16,4,48,1320]{3,2,1,0:T(8,128)(2,1)} %all-gather.5.cloned.1.call-done.g_ref, f32[256,1320]{1,0:T(8,128)} %half.4.part_ref), custom_call_target="tpu_custom_call" | custom-call | tf_op jit(solution)/shard_map/update/pallas_call | solution.py:281
  214.1 4.9 project.11
  219.5 4.9 project.10.k_ref
  228.6 9.6 %collective-permute-done.10.f_ref = bf16[256,768]{1,0:T(8,128)(2,1)S(1)} collective-permute-done((bf16[256,768]{1,0:T(8,128)(2,1)S(1)}, bf16[256,768]{1,0:T(8,128)(2,1)S(1)}, u32[]{:S(2)}, u32[]{:S(2)}) %collective-permute-start.10) | collective-permute-done | bytes 393248 | tf_op jit(solution)/shard_map/ppermute | solution.py:386
  242.0 32.0 %collective-permute-start.11 = (bf16[256,672]{1,0:T(8,128)(2,1)}, bf16[256,672]{1,0:T(8,128)(2,1)S(1)}, u32[]{:S(2)}, u32[]{:S(2)}) collective-permute-start(bf16[256,672]{1,0:T(8,128)(2,1)} %get-tuple-element.26.v0_ref.v_ref), channel_id=1, source_target_pairs={{0,8},{4,12},{8,16},{12,20},{16,24},{20,28},{24,32},{28,36},{32,40... | collective-permute-start | bytes 1032200 | tf_op jit(solution)/shard_map/ppermute | solution.py:391
  275.9 6.0 %collective-permute-done.11.v2_ref = bf16[256,672]{1,0:T(8,128)(2,1)S(1)} collective-permute-done((bf16[256,672]{1,0:T(8,128)(2,1)}, bf16[256,672]{1,0:T(8,128)(2,1)S(1)}, u32[]{:S(2)}, u32[]{:S(2)}) %collective-permute-start.11) | collective-permute-done | bytes 344096 | tf_op jit(solution)/shard_map/ppermute | solution.py:391
  281.9 4.0 collective-permute-done.12.v1_ref
  286.7 4.5 attend.3.a_ref
  294.6 8.4 %collective-permute-done.13.a_ref = bf16[256,768]{1,0:T(8,128)(2,1)S(1)} collective-permute-done((bf16[256,768]{1,0:T(8,128)(2,1)}, bf16[256,768]{1,0:T(8,128)(2,1)S(1)}, u32[]{:S(2)}, u32[]{:S(2)}) %collective-permute-start.13) | collective-permute-done | bytes 393248 | tf_op jit(solution)/shard_map/ppermute | solution.py:386
  303.1 4.2 all_to_all.33
  309.3 5.9 %half.5.part_ref = f32[256,1320]{1,0:T(8,128)} custom-call(s32[2]{0:T(128)} %pad_add_fusion.1.sel, bf16[256,768]{1,0:T(8,128)(2,1)} %attend.3.a_ref, bf16[256,768]{1,0:T(8,128)(2,1)} %copy-done.18, bf16[16,4,48,1320]{3,2,1,0:T(8,128)(2,1)} %all-gather.5.cloned.1.call-done.g_ref, f32[256,1320]{1,0:T(8,128)} %get-tuple-element.27.base_ref.cur_ref), custom_call_target="tpu_custom_call" | custom-call | tf_op jit(solution)/shard_map/half/pallas_call | solution.py:243
  316.0 6.3 %update.3 = (f32[256,1320]{1,0:T(8,128)}, bf16[256,1320]{1,0:T(8,128)(2,1)}, f32[256,1]{1,0:T(8,128)}) custom-call(s32[2]{0:T(128)} %pad_add_fusion.sel, bf16[256,768]{1,0:T(8,128)(2,1)} %copy-done.15, bf16[256,768]{1,0:T(8,128)(2,1)} %copy-done.16, bf16[16,4,48,1320]{3,2,1,0:T(8,128)(2,1)} %all-gather.5.cloned.1.call-done.g_ref, f32[256,1320]{1,0:T(8,128)} %half.5.part_ref), custom_call_target="tpu_custom_call" | custom-call | tf_op jit(solution)/shard_map/update/pallas_call | solution.py:281
  322.3 4.9 project.13
  327.5 4.9 project.12.k_ref
  337.0 9.6 %collective-permute-done.20.f_ref = bf16[256,768]{1,0:T(8,128)(2,1)S(1)} collective-permute-done((bf16[256,768]{1,0:T(8,128)(2,1)S(1)}, bf16[256,768]{1,0:T(8,128)(2,1)S(1)}, u32[]{:S(2)}, u32[]{:S(2)}) %collective-permute-start.20) | collective-permute-done | bytes 393248 | tf_op jit(solution)/shard_map/ppermute | solution.py:386
  347.4 4.7 spread.2
  355.3 9.4 %collective-permute-done.21.r1_ref = bf16[256,672]{1,0:T(8,128)(2,1)S(1)} collective-permute-done((bf16[256,672]{1,0:T(8,128)(2,1)}, bf16[256,672]{1,0:T(8,128)(2,1)S(1)}, u32[]{:S(2)}, u32[]{:S(2)}) %collective-permute-start.21) | collective-permute-done | bytes 344096 | tf_op jit(solution)/shard_map/ppermute | solution.py:391
  364.8 11.9 %collective-permute-done.22.r2_ref = bf16[256,672]{1,0:T(8,128)(2,1)S(1)} collective-permute-done((bf16[256,672]{1,0:T(8,128)(2,1)}, bf16[256,672]{1,0:T(8,128)(2,1)S(1)}, u32[]{:S(2)}, u32[]{:S(2)}) %collective-permute-start.22) | collective-permute-done | bytes 344096 | tf_op jit(solution)/shard_map/ppermute | solution.py:391
  383.9 8.4 %collective-permute-done.23.a_ref = bf16[256,768]{1,0:T(8,128)(2,1)S(1)} collective-permute-done((bf16[256,768]{1,0:T(8,128)(2,1)}, bf16[256,768]{1,0:T(8,128)(2,1)S(1)}, u32[]{:S(2)}, u32[]{:S(2)}) %collective-permute-start.23) | collective-permute-done | bytes 393248 | tf_op jit(solution)/shard_map/ppermute | solution.py:386
  394.9 5.9 %half.6.part_ref = f32[256,1320]{1,0:T(8,128)} custom-call(s32[2]{0:T(128)} %pad_add_fusion.1.sel, bf16[256,768]{1,0:T(8,128)(2,1)} %gather_grad.2.a_ref.c_ref, bf16[256,768]{1,0:T(8,128)(2,1)} %copy-done.9, bf16[16,4,48,1320]{3,2,1,0:T(8,128)(2,1)} %all-gather.3.cloned.1.call-done.g_ref, f32[256,1320]{1,0:T(8,128)} %broadcast_in_dim.20.base_ref), custom_call_target="tpu_custom_call" | custom-call | tf_op jit(solution)/shard_map/half/pallas_call | solution.py:243
  401.6 7.5 %backstep.2 = (f32[256,1320]{1,0:T(8,128)}, bf16[256,1320]{1,0:T(8,128)(2,1)}) custom-call(s32[2]{0:T(128)} %pad_add_fusion.sel, bf16[256,768]{1,0:T(8,128)(2,1)} %copy-done.34, bf16[256,768]{1,0:T(8,128)(2,1)} %copy-done.35, bf16[256,768]{1,0:T(8,128)(2,1)} %gather_grad.2.a_ref.c_ref, bf16[256,768]{1,0:T(8,128)(2,1)} %copy-done.9, ...), custom_call_target="tpu_custom_call" | custom-call | tf_op jit(solution)/shard_map/backstep/pallas_call | solution.py:329
  409.1 4.8 project.15
  414.4 4.9 project.14.k_ref
  423.9 9.3 %collective-permute-done.27.f_ref = bf16[256,768]{1,0:T(8,128)(2,1)S(1)} collective-permute-done((bf16[256,768]{1,0:T(8,128)(2,1)S(1)}, bf16[256,768]{1,0:T(8,128)(2,1)S(1)}, u32[]{:S(2)}, u32[]{:S(2)}) %collective-permute-start.27) | collective-permute-done | bytes 393248 | tf_op jit(solution)/shard_map/ppermute | solution.py:386
  433.9 4.7 spread.3
  441.9 15.8 %collective-permute-done.28.r1_ref = bf16[256,672]{1,0:T(8,128)(2,1)S(1)} collective-permute-done((bf16[256,672]{1,0:T(8,128)(2,1)}, bf16[256,672]{1,0:T(8,128)(2,1)S(1)}, u32[]{:S(2)}, u32[]{:S(2)}) %collective-permute-start.28) | collective-permute-done | bytes 344096 | tf_op jit(solution)/shard_map/ppermute | solution.py:391
  457.7 9.0 %collective-permute-done.29.r2_ref = bf16[256,672]{1,0:T(8,128)(2,1)S(1)} collective-permute-done((bf16[256,672]{1,0:T(8,128)(2,1)}, bf16[256,672]{1,0:T(8,128)(2,1)S(1)}, u32[]{:S(2)}, u32[]{:S(2)}) %collective-permute-start.29) | collective-permute-done | bytes 344096 | tf_op jit(solution)/shard_map/ppermute | solution.py:391
  473.8 7.8 %collective-permute-done.30.a_ref = bf16[256,768]{1,0:T(8,128)(2,1)S(1)} collective-permute-done((bf16[256,768]{1,0:T(8,128)(2,1)}, bf16[256,768]{1,0:T(8,128)(2,1)S(1)}, u32[]{:S(2)}, u32[]{:S(2)}) %collective-permute-start.30) | collective-permute-done | bytes 393248 | tf_op jit(solution)/shard_map/ppermute | solution.py:386
  483.3 5.9 %half.7.part_ref = f32[256,1320]{1,0:T(8,128)} custom-call(s32[2]{0:T(128)} %pad_add_fusion.1.sel, bf16[256,768]{1,0:T(8,128)(2,1)} %gather_grad.3.a_ref.c_ref, bf16[256,768]{1,0:T(8,128)(2,1)} %copy-done.8, bf16[16,4,48,1320]{3,2,1,0:T(8,128)(2,1)} %all-gather.3.cloned.1.call-done.g_ref, f32[256,1320]{1,0:T(8,128)} %broadcast_in_dim.20.base_ref), custom_call_target="tpu_custom_call" | custom-call | tf_op jit(solution)/shard_map/half/pallas_call | solution.py:243
  490.0 7.5 %backstep.3 = (f32[256,1320]{1,0:T(8,128)}, bf16[256,1320]{1,0:T(8,128)(2,1)}) custom-call(s32[2]{0:T(128)} %pad_add_fusion.sel, bf16[256,768]{1,0:T(8,128)(2,1)} %copy-done.32, bf16[256,768]{1,0:T(8,128)(2,1)} %copy-done.33, bf16[256,768]{1,0:T(8,128)(2,1)} %gather_grad.3.a_ref.c_ref, bf16[256,768]{1,0:T(8,128)(2,1)} %copy-done.8, ...), custom_call_target="tpu_custom_call" | custom-call | tf_op jit(solution)/shard_map/backstep/pallas_call | solution.py:329
  505.9 5.7 %collective-permute-done.17.c_ref = bf16[128,1320]{1,0:T(8,128)(2,1)S(1)} collective-permute-done((bf16[128,1320]{1,0:T(8,128)(2,1)S(1)}, bf16[128,1320]{1,0:T(8,128)(2,1)S(1)}, u32[]{:S(2)}, u32[]{:S(2)}) %collective-permute-start.17) | collective-permute-done | bytes 337952 | tf_op jit(solution)/shard_map/ppermute | solution.py:386
  511.6 7.7 %collective-permute-done.18.d_ref = bf16[128,1320]{1,0:T(8,128)(2,1)S(1)} collective-permute-done((bf16[128,1320]{1,0:T(8,128)(2,1)S(1)}, bf16[128,1320]{1,0:T(8,128)(2,1)S(1)}, u32[]{:S(2)}, u32[]{:S(2)}) %collective-permute-start.18) | collective-permute-done | bytes 337952 | tf_op jit(solution)/shard_map/ppermute | solution.py:386
  527.1 7.2 %collective-permute-done.35.d_ref = bf16[128,1320]{1,0:T(8,128)(2,1)S(1)} collective-permute-done((bf16[128,1320]{1,0:T(8,128)(2,1)S(1)}, bf16[128,1320]{1,0:T(8,128)(2,1)S(1)}, u32[]{:S(2)}, u32[]{:S(2)}) %collective-permute-start.35) | collective-permute-done | bytes 337952 | tf_op jit(solution)/shard_map/ppermute | solution.py:386
  (201 shorter events, 117.5 us)
Async XLA Ops:
  7.2 30.8 %copy-start = (bf16[128,5280]{0,1:T(8,128)(2,1)S(1)}, bf16[128,5280]{0,1:T(8,128)(2,1)}, u32[]{:S(2)}) copy-start(bf16[128,5280]{0,1:T(8,128)(2,1)} %param.7) | copy-start | bytes 4055044
  7.2 88.7 %all-gather.3.cloned.1.call-start = ((), (), s32[]{:S(2)}) async-start(), calls=%async_computation.6 | async-start | bytes 9191424 | tf_op jit(solution)/shard_map/all_gather | solution.py:444
  23.8 176.6 %all-gather.5.cloned.1.call-start = ((), (), s32[]{:S(2)}) async-start(), calls=%async_computation.7 | async-start | bytes 9191424 | tf_op jit(solution)/shard_map/all_gather | solution.py:446
  38.9 5.4 all-to-all-start.2
  100.9 16.7 %collective-permute-start.2 = (bf16[2,256,768]{2,1,0:T(8,128)(2,1)}, bf16[2,256,768]{2,1,0:T(8,128)(2,1)S(1)}, u32[]{:S(2)}, u32[]{:S(2)}) collective-permute-start(bf16[2,256,768]{2,1,0:T(8,128)(2,1)} %project.9), channel_id=1, source_target_pairs={{0,2},{2,0},{1,3},{3,1},{4,6},{6,4},{5,7},{7,5},{8,10},{10,8},{9,1... | collective-permute-start | bytes 2359304 | tf_op jit(solution)/shard_map/ppermute | solution.py:382
  105.1 64.2 %collective-permute-start = (bf16[256,672]{1,0:T(8,128)(2,1)S(1)}, bf16[256,672]{1,0:T(8,128)(2,1)S(1)}, u32[]{:S(2)}, u32[]{:S(2)}) collective-permute-start(bf16[256,672]{1,0:T(8,128)(2,1)S(1)} %bitcast.55), channel_id=1, source_target_pairs={{0,8},{4,12},{8,16},{12,20},{16,24},{20,28},{24,32},{28,36},{32,40... | collective-permute-start | bytes 1032200 | tf_op jit(solution)/shard_map/ppermute | solution.py:391
  109.3 60.0 %collective-permute-start.1 = (bf16[256,672]{1,0:T(8,128)(2,1)S(1)}, bf16[256,672]{1,0:T(8,128)(2,1)S(1)}, u32[]{:S(2)}, u32[]{:S(2)}) collective-permute-start(bf16[256,672]{1,0:T(8,128)(2,1)S(1)} %bitcast.56), channel_id=1, source_target_pairs={{0,4},{4,8},{8,12},{12,16},{16,20},{20,24},{24,28},{28,32},{32,36}... | collective-permute-start | bytes 1032200 | tf_op jit(solution)/shard_map/ppermute | solution.py:391
  119.0 12.2 %collective-permute-start.3 = (bf16[256,768]{1,0:T(8,128)(2,1)S(1)}, bf16[256,768]{1,0:T(8,128)(2,1)S(1)}, u32[]{:S(2)}, u32[]{:S(2)}) collective-permute-start(bf16[256,768]{1,0:T(8,128)(2,1)S(1)} %fusion.5), channel_id=1, source_target_pairs={{0,1},{1,0},{2,3},{3,2},{4,5},{5,4},{6,7},{7,6},{8,9},{9,8},{10,11... | collective-permute-start | bytes 1179656 | tf_op jit(solution)/shard_map/ppermute | solution.py:386
  123.5 43.1 %copy-start.47 = (s32[64]{0:T(128)S(1)}, s32[64]{0:T(128)}, u32[]{:S(2)}) copy-start(s32[64]{0:T(128)} %param.12) | copy-start | bytes 772
  134.8 43.9 %collective-permute-start.4 = (bf16[256,672]{1,0:T(8,128)(2,1)}, bf16[256,672]{1,0:T(8,128)(2,1)S(1)}, u32[]{:S(2)}, u32[]{:S(2)}) collective-permute-start(bf16[256,672]{1,0:T(8,128)(2,1)} %get-tuple-element.23.v0_ref.v_ref), channel_id=1, source_target_pairs={{0,8},{4,12},{8,16},{12,20},{16,24},{20,28},{24,32},{28,36},{32,40... | collective-permute-start | bytes 1032200 | tf_op jit(solution)/shard_map/ppermute | solution.py:391
  161.2 21.7 %collective-permute-start.5 = (bf16[256,672]{1,0:T(8,128)(2,1)}, bf16[256,672]{1,0:T(8,128)(2,1)S(1)}, u32[]{:S(2)}, u32[]{:S(2)}) collective-permute-start(bf16[256,672]{1,0:T(8,128)(2,1)} %get-tuple-element.23.v0_ref.v_ref), channel_id=1, source_target_pairs={{0,4},{4,8},{8,12},{12,16},{16,20},{20,24},{24,28},{28,32},{32,36}... | collective-permute-start | bytes 1032200 | tf_op jit(solution)/shard_map/ppermute | solution.py:391
  163.1 5.2 all-to-all-start
  183.7 15.4 %copy-start.2 = (bf16[2,128,1320]{2,1,0:T(8,128)(2,1)S(1)}, bf16[2,128,1320]{2,1,0:T(8,128)(2,1)}, u32[]{:S(2)}) copy-start(bf16[2,128,1320]{2,1,0:T(8,128)(2,1)} %copy.29) | copy-start | bytes 2027524
  188.4 10.6 %collective-permute-start.6 = (bf16[256,768]{1,0:T(8,128)(2,1)}, bf16[256,768]{1,0:T(8,128)(2,1)S(1)}, u32[]{:S(2)}, u32[]{:S(2)}) collective-permute-start(bf16[256,768]{1,0:T(8,128)(2,1)} %attend.2.a_ref), channel_id=1, source_target_pairs={{0,1},{1,0},{2,3},{3,2},{4,5},{5,4},{6,7},{7,6},{8,9},{9,8},{10,11... | collective-permute-start | bytes 1179656 | tf_op jit(solution)/shard_map/ppermute | solution.py:386
  192.3 8.0 %collective-permute-start.8 = (bf16[256,768]{1,0:T(8,128)(2,1)}, bf16[256,768]{1,0:T(8,128)(2,1)S(1)}, u32[]{:S(2)}, u32[]{:S(2)}) collective-permute-start(bf16[256,768]{1,0:T(8,128)(2,1)} %attend.2.a_ref), channel_id=1, source_target_pairs={{0,2},{2,0},{1,3},{3,1},{4,6},{6,4},{5,7},{7,5},{8,10},{10,8},{9,1... | collective-permute-start | bytes 1179656 | tf_op jit(solution)/shard_map/ppermute | solution.py:382
  198.9 8.1 %collective-permute-start.7 = (bf16[256,768]{1,0:T(8,128)(2,1)S(1)}, bf16[256,768]{1,0:T(8,128)(2,1)S(1)}, u32[]{:S(2)}, u32[]{:S(2)}) collective-permute-start(bf16[256,768]{1,0:T(8,128)(2,1)S(1)} %collective-permute-done.6.a_ref), channel_id=1, source_target_pairs={{0,2},{2,0},{1,3},{3,1},{4,6},{6,4},{5,7},{7,5},{8,10},{10,8},{9,1... | collective-permute-start | bytes 1179656 | tf_op jit(solution)/shard_map/ppermute | solution.py:382
  219.0 5.4 collective-permute-start.9
  225.6 12.6 %collective-permute-start.10 = (bf16[256,768]{1,0:T(8,128)(2,1)S(1)}, bf16[256,768]{1,0:T(8,128)(2,1)S(1)}, u32[]{:S(2)}, u32[]{:S(2)}) collective-permute-start(bf16[256,768]{1,0:T(8,128)(2,1)S(1)} %fusion.4), channel_id=1, source_target_pairs={{0,1},{1,0},{2,3},{3,2},{4,5},{5,4},{6,7},{7,6},{8,9},{9,8},{10,11... | collective-permute-start | bytes 1179656 | tf_op jit(solution)/shard_map/ppermute | solution.py:386
  242.0 61.0 %copy-start.45 = (bf16[128,5280]{0,1:T(8,128)(2,1)S(1)}, bf16[128,5280]{0,1:T(8,128)(2,1)}, u32[]{:S(2)}) copy-start(bf16[128,5280]{0,1:T(8,128)(2,1)} %param.13) | copy-start | bytes 4055044
  242.0 39.9 %collective-permute-start.11 = (bf16[256,672]{1,0:T(8,128)(2,1)}, bf16[256,672]{1,0:T(8,128)(2,1)S(1)}, u32[]{:S(2)}, u32[]{:S(2)}) collective-permute-start(bf16[256,672]{1,0:T(8,128)(2,1)} %get-tuple-element.26.v0_ref.v_ref), channel_id=1, source_target_pairs={{0,8},{4,12},{8,16},{12,20},{16,24},{20,28},{24,32},{28,36},{32,40... | collective-permute-start | bytes 1032200 | tf_op jit(solution)/shard_map/ppermute | solution.py:391
  274.0 12.0 %collective-permute-start.12 = (bf16[256,672]{1,0:T(8,128)(2,1)}, bf16[256,672]{1,0:T(8,128)(2,1)S(1)}, u32[]{:S(2)}, u32[]{:S(2)}) collective-permute-start(bf16[256,672]{1,0:T(8,128)(2,1)} %get-tuple-element.26.v0_ref.v_ref), channel_id=1, source_target_pairs={{0,4},{4,8},{8,12},{12,16},{16,20},{20,24},{24,28},{28,32},{32,36}... | collective-permute-start | bytes 1032200 | tf_op jit(solution)/shard_map/ppermute | solution.py:391
  291.2 11.7 %collective-permute-start.13 = (bf16[256,768]{1,0:T(8,128)(2,1)}, bf16[256,768]{1,0:T(8,128)(2,1)S(1)}, u32[]{:S(2)}, u32[]{:S(2)}) collective-permute-start(bf16[256,768]{1,0:T(8,128)(2,1)} %attend.3.a_ref), channel_id=1, source_target_pairs={{0,1},{1,0},{2,3},{3,2},{4,5},{5,4},{6,7},{7,6},{8,9},{9,8},{10,11... | collective-permute-start | bytes 1179656 | tf_op jit(solution)/shard_map/ppermute | solution.py:386
  294.6 13.9 %collective-permute-start.15 = (bf16[256,768]{1,0:T(8,128)(2,1)}, bf16[256,768]{1,0:T(8,128)(2,1)S(1)}, u32[]{:S(2)}, u32[]{:S(2)}) collective-permute-start(bf16[256,768]{1,0:T(8,128)(2,1)} %attend.3.a_ref), channel_id=1, source_target_pairs={{0,2},{2,0},{1,3},{3,1},{4,6},{6,4},{5,7},{7,5},{8,10},{10,8},{9,1... | collective-permute-start | bytes 1179656 | tf_op jit(solution)/shard_map/ppermute | solution.py:382
  303.0 12.2 %collective-permute-start.14 = (bf16[256,768]{1,0:T(8,128)(2,1)S(1)}, bf16[256,768]{1,0:T(8,128)(2,1)S(1)}, u32[]{:S(2)}, u32[]{:S(2)}) collective-permute-start(bf16[256,768]{1,0:T(8,128)(2,1)S(1)} %collective-permute-done.13.a_ref), channel_id=1, source_target_pairs={{0,2},{2,0},{1,3},{3,1},{4,6},{6,4},{5,7},{7,5},{8,10},{10,8},{9,1... | collective-permute-start | bytes 1179656 | tf_op jit(solution)/shard_map/ppermute | solution.py:382
  327.1 5.2 collective-permute-start.19
  333.6 13.0 %collective-permute-start.20 = (bf16[256,768]{1,0:T(8,128)(2,1)S(1)}, bf16[256,768]{1,0:T(8,128)(2,1)S(1)}, u32[]{:S(2)}, u32[]{:S(2)}) collective-permute-start(bf16[256,768]{1,0:T(8,128)(2,1)S(1)} %fusion.3), channel_id=1, source_target_pairs={{0,1},{1,0},{2,3},{3,2},{4,5},{5,4},{6,7},{7,6},{8,9},{9,8},{10,11... | collective-permute-start | bytes 1179656 | tf_op jit(solution)/shard_map/ppermute | solution.py:386
  352.1 12.6 %collective-permute-start.21 = (bf16[256,672]{1,0:T(8,128)(2,1)}, bf16[256,672]{1,0:T(8,128)(2,1)S(1)}, u32[]{:S(2)}, u32[]{:S(2)}) collective-permute-start(bf16[256,672]{1,0:T(8,128)(2,1)} %get-tuple-element.32), channel_id=1, source_target_pairs={{4,0},{8,4},{12,8},{16,12},{20,16},{24,20},{28,24},{32,28},{36,32}... | collective-permute-start | bytes 1032200 | tf_op jit(solution)/shard_map/ppermute | solution.py:391
  354.0 22.7 %collective-permute-start.22 = (bf16[256,672]{1,0:T(8,128)(2,1)}, bf16[256,672]{1,0:T(8,128)(2,1)S(1)}, u32[]{:S(2)}, u32[]{:S(2)}) collective-permute-start(bf16[256,672]{1,0:T(8,128)(2,1)} %get-tuple-element.33), channel_id=1, source_target_pairs={{8,0},{12,4},{16,8},{20,12},{24,16},{28,20},{32,24},{36,28},{40,32... | collective-permute-start | bytes 1032200 | tf_op jit(solution)/shard_map/ppermute | solution.py:391
  380.6 11.7 %collective-permute-start.23 = (bf16[256,768]{1,0:T(8,128)(2,1)}, bf16[256,768]{1,0:T(8,128)(2,1)S(1)}, u32[]{:S(2)}, u32[]{:S(2)}) collective-permute-start(bf16[256,768]{1,0:T(8,128)(2,1)} %gather_grad.2.a_ref.c_ref), channel_id=1, source_target_pairs={{0,1},{1,0},{2,3},{3,2},{4,5},{5,4},{6,7},{7,6},{8,9},{9,8},{10,11... | collective-permute-start | bytes 1179656 | tf_op jit(solution)/shard_map/ppermute | solution.py:386
  383.9 9.8 %collective-permute-start.25 = (bf16[256,768]{1,0:T(8,128)(2,1)}, bf16[256,768]{1,0:T(8,128)(2,1)S(1)}, u32[]{:S(2)}, u32[]{:S(2)}) collective-permute-start(bf16[256,768]{1,0:T(8,128)(2,1)} %gather_grad.2.a_ref.c_ref), channel_id=1, source_target_pairs={{0,2},{2,0},{1,3},{3,1},{4,6},{6,4},{5,7},{7,5},{8,10},{10,8},{9,1... | collective-permute-start | bytes 1179656 | tf_op jit(solution)/shard_map/ppermute | solution.py:382
  392.3 8.5 %collective-permute-start.24 = (bf16[256,768]{1,0:T(8,128)(2,1)S(1)}, bf16[256,768]{1,0:T(8,128)(2,1)S(1)}, u32[]{:S(2)}, u32[]{:S(2)}) collective-permute-start(bf16[256,768]{1,0:T(8,128)(2,1)S(1)} %collective-permute-done.23.a_ref), channel_id=1, source_target_pairs={{0,2},{2,0},{1,3},{3,1},{4,6},{6,4},{5,7},{7,5},{8,10},{10,8},{9,1... | collective-permute-start | bytes 1179656 | tf_op jit(solution)/shard_map/ppermute | solution.py:382
  413.9 5.4 collective-permute-start.26
  420.6 12.6 %collective-permute-start.27 = (bf16[256,768]{1,0:T(8,128)(2,1)S(1)}, bf16[256,768]{1,0:T(8,128)(2,1)S(1)}, u32[]{:S(2)}, u32[]{:S(2)}) collective-permute-start(bf16[256,768]{1,0:T(8,128)(2,1)S(1)} %fusion.2), channel_id=1, source_target_pairs={{0,1},{1,0},{2,3},{3,2},{4,5},{5,4},{6,7},{7,6},{8,9},{9,8},{10,11... | collective-permute-start | bytes 1179656 | tf_op jit(solution)/shard_map/ppermute | solution.py:386
  438.7 19.1 %collective-permute-start.28 = (bf16[256,672]{1,0:T(8,128)(2,1)}, bf16[256,672]{1,0:T(8,128)(2,1)S(1)}, u32[]{:S(2)}, u32[]{:S(2)}) collective-permute-start(bf16[256,672]{1,0:T(8,128)(2,1)} %get-tuple-element.37), channel_id=1, source_target_pairs={{4,0},{8,4},{12,8},{16,12},{20,16},{24,20},{28,24},{32,28},{36,32}... | collective-permute-start | bytes 1032200 | tf_op jit(solution)/shard_map/ppermute | solution.py:391
  440.6 26.1 %collective-permute-start.29 = (bf16[256,672]{1,0:T(8,128)(2,1)}, bf16[256,672]{1,0:T(8,128)(2,1)S(1)}, u32[]{:S(2)}, u32[]{:S(2)}) collective-permute-start(bf16[256,672]{1,0:T(8,128)(2,1)} %get-tuple-element.38), channel_id=1, source_target_pairs={{8,0},{12,4},{16,8},{20,12},{24,16},{28,20},{32,24},{36,28},{40,32... | collective-permute-start | bytes 1032200 | tf_op jit(solution)/shard_map/ppermute | solution.py:391
  470.6 11.0 %collective-permute-start.30 = (bf16[256,768]{1,0:T(8,128)(2,1)}, bf16[256,768]{1,0:T(8,128)(2,1)S(1)}, u32[]{:S(2)}, u32[]{:S(2)}) collective-permute-start(bf16[256,768]{1,0:T(8,128)(2,1)} %gather_grad.3.a_ref.c_ref), channel_id=1, source_target_pairs={{0,1},{1,0},{2,3},{3,2},{4,5},{5,4},{6,7},{7,6},{8,9},{9,8},{10,11... | collective-permute-start | bytes 1179656 | tf_op jit(solution)/shard_map/ppermute | solution.py:386
  473.8 8.7 %collective-permute-start.32 = (bf16[256,768]{1,0:T(8,128)(2,1)}, bf16[256,768]{1,0:T(8,128)(2,1)S(1)}, u32[]{:S(2)}, u32[]{:S(2)}) collective-permute-start(bf16[256,768]{1,0:T(8,128)(2,1)} %gather_grad.3.a_ref.c_ref), channel_id=1, source_target_pairs={{0,2},{2,0},{1,3},{3,1},{4,6},{6,4},{5,7},{7,5},{8,10},{10,8},{9,1... | collective-permute-start | bytes 1179656 | tf_op jit(solution)/shard_map/ppermute | solution.py:382
  481.6 7.6 %collective-permute-start.31 = (bf16[256,768]{1,0:T(8,128)(2,1)S(1)}, bf16[256,768]{1,0:T(8,128)(2,1)S(1)}, u32[]{:S(2)}, u32[]{:S(2)}) collective-permute-start(bf16[256,768]{1,0:T(8,128)(2,1)S(1)} %collective-permute-done.30.a_ref), channel_id=1, source_target_pairs={{0,2},{2,0},{1,3},{3,1},{4,6},{6,4},{5,7},{7,5},{8,10},{10,8},{9,1... | collective-permute-start | bytes 1179656 | tf_op jit(solution)/shard_map/ppermute | solution.py:382
  481.7 17.1 %copy-start.11 = (bf16[128,1320]{1,0:T(8,128)(2,1)}, bf16[128,1320]{1,0:T(8,128)(2,1)S(1)}, u32[]{:S(2)}) copy-start(bf16[128,1320]{1,0:T(8,128)(2,1)S(1)} %get-tuple-element.51.a_ref) | copy-start | bytes 1013764
  481.7 20.2 %collective-permute-start.16 = (bf16[128,1320]{1,0:T(8,128)(2,1)S(1)}, bf16[128,1320]{1,0:T(8,128)(2,1)S(1)}, u32[]{:S(2)}, u32[]{:S(2)}) collective-permute-start(bf16[128,1320]{1,0:T(8,128)(2,1)S(1)} %get-tuple-element.50), channel_id=1, source_target_pairs={{0,2},{2,0},{1,3},{3,1},{4,6},{6,4},{5,7},{7,5},{8,10},{10,8},{9,1... | collective-permute-start | bytes 1013768 | tf_op jit(solution)/shard_map/ppermute | solution.py:382
  498.7 26.7 %copy-start.12 = (bf16[128,1320]{1,0:T(8,128)(2,1)}, bf16[128,1320]{1,0:T(8,128)(2,1)S(1)}, u32[]{:S(2)}) copy-start(bf16[128,1320]{1,0:T(8,128)(2,1)S(1)} %get-tuple-element.49.a_ref) | copy-start | bytes 1013764
  498.7 6.8 %collective-permute-start.33 = (bf16[128,1320]{1,0:T(8,128)(2,1)S(1)}, bf16[128,1320]{1,0:T(8,128)(2,1)S(1)}, u32[]{:S(2)}, u32[]{:S(2)}) collective-permute-start(bf16[128,1320]{1,0:T(8,128)(2,1)S(1)} %get-tuple-element.48), channel_id=1, source_target_pairs={{0,2},{2,0},{1,3},{3,1},{4,6},{6,4},{5,7},{7,5},{8,10},{10,8},{9,1... | collective-permute-start | bytes 1013768 | tf_op jit(solution)/shard_map/ppermute | solution.py:382
  498.8 12.9 %collective-permute-start.17 = (bf16[128,1320]{1,0:T(8,128)(2,1)S(1)}, bf16[128,1320]{1,0:T(8,128)(2,1)S(1)}, u32[]{:S(2)}, u32[]{:S(2)}) collective-permute-start(bf16[128,1320]{1,0:T(8,128)(2,1)S(1)} %get-tuple-element.51.a_ref), channel_id=1, source_target_pairs={{0,1},{1,0},{2,3},{3,2},{4,5},{5,4},{6,7},{7,6},{8,9},{9,8},{10,11... | collective-permute-start | bytes 1013768 | tf_op jit(solution)/shard_map/ppermute | solution.py:386
  502.0 17.4 %copy-start.38 = (bf16[128,1320]{1,0:T(8,128)(2,1)}, bf16[128,1320]{1,0:T(8,128)(2,1)S(1)}, u32[]{:S(2)}) copy-start(bf16[128,1320]{1,0:T(8,128)(2,1)S(1)} %collective-permute-done.16.b_ref) | copy-start | bytes 1013764
  502.0 17.4 %collective-permute-start.18 = (bf16[128,1320]{1,0:T(8,128)(2,1)S(1)}, bf16[128,1320]{1,0:T(8,128)(2,1)S(1)}, u32[]{:S(2)}, u32[]{:S(2)}) collective-permute-start(bf16[128,1320]{1,0:T(8,128)(2,1)S(1)} %collective-permute-done.16.b_ref), channel_id=1, source_target_pairs={{0,1},{1,0},{2,3},{3,2},{4,5},{5,4},{6,7},{7,6},{8,9},{9,8},{10,11... | collective-permute-start | bytes 1013768 | tf_op jit(solution)/shard_map/ppermute | solution.py:386
  502.4 24.7 %collective-permute-start.34 = (bf16[128,1320]{1,0:T(8,128)(2,1)S(1)}, bf16[128,1320]{1,0:T(8,128)(2,1)S(1)}, u32[]{:S(2)}, u32[]{:S(2)}) collective-permute-start(bf16[128,1320]{1,0:T(8,128)(2,1)S(1)} %get-tuple-element.49.a_ref), channel_id=1, source_target_pairs={{0,1},{1,0},{2,3},{3,2},{4,5},{5,4},{6,7},{7,6},{8,9},{9,8},{10,11... | collective-permute-start | bytes 1013768 | tf_op jit(solution)/shard_map/ppermute | solution.py:386
  505.5 28.8 %copy-start.41 = (bf16[128,1320]{1,0:T(8,128)(2,1)}, bf16[128,1320]{1,0:T(8,128)(2,1)S(1)}, u32[]{:S(2)}) copy-start(bf16[128,1320]{1,0:T(8,128)(2,1)S(1)} %collective-permute-done.33.b_ref) | copy-start | bytes 1013764
  505.5 28.8 %collective-permute-start.35 = (bf16[128,1320]{1,0:T(8,128)(2,1)S(1)}, bf16[128,1320]{1,0:T(8,128)(2,1)S(1)}, u32[]{:S(2)}, u32[]{:S(2)}) collective-permute-start(bf16[128,1320]{1,0:T(8,128)(2,1)S(1)} %collective-permute-done.33.b_ref), channel_id=1, source_target_pairs={{0,1},{1,0},{2,3},{3,2},{4,5},{5,4},{6,7},{7,6},{8,9},{9,8},{10,11... | collective-permute-start | bytes 1013768 | tf_op jit(solution)/shard_map/ppermute | solution.py:386
  (40 other events, 207.6 us)
Sparse Core Ops, SparseCore 0:
  23.9 71.9 all-gather.2
  98.1 98.1 all-gather.4
